TPU v7x, 768 devices: a whole 4x8x12 slice. The times are simulated.
768 devices in a mesh: dom: 192 (over y, z, core), sub: 4 (over x).
Axes of the slice: x: 4, y: 8, z: 12, core: 2. Of those that a mesh axis runs over, the one named last changes fastest.
Arguments:
- dof_state: float32 [56, 9, 98304], P(None, None, ('dom', 'sub')), may hold values from -6 to 6
- stiffness: float32 [3, 56, 56], replicated, may hold values from -0.75 to 0.75
- face_proj: float32 [4, 21, 56], replicated, may hold values from -0.75 to 0.75
- face_lift: float32 [4, 56, 21], replicated, may hold values from -1 to 1
- face_rotate: float32 [3, 21, 21], replicated, may hold values from -1.25 to 1.25
- jacobians: float32 [16, 3, 9, 9], replicated, may hold values from -2 to 2
- material: int32 [98304], P(('dom', 'sub')), may hold values from 0 to 15
- inv_jacobian: float32 [3, 3, 98304], P(None, None, ('dom', 'sub')), may hold values from -2.5 to 2.5
- flux_own: float32 [4, 9, 9, 98304], P(None, None, None, ('dom', 'sub')), may hold values from -1.5 to 1.5
- flux_across: float32 [4, 9, 9, 98304], P(None, None, None, ('dom', 'sub')), may hold values from -1.5 to 1.5
- cluster: int32 [98304], P(('dom', 'sub')), may hold values from 0 to 1, as said below
- neighbour: int32 [4, 98304], P(None, ('dom', 'sub')), may hold values from 0 to 224, as said below
- across_face: int32 [4, 98304], P(None, ('dom', 'sub')), may hold values from 0 to 3
- rotation: int32 [4, 98304], P(None, ('dom', 'sub')), may hold values from 0 to 2
- send_list: int32 [73728], P(('dom', 'sub')), may hold values from 0 to 127
Outputs:
- dof_out: float32 [56, 9, 98304], P(None, None, ('dom', 'sub'))
Inputs may be any that keep to these rules, and one draw needn't show every extreme that they name: `cluster`: each partition of 128 elements has at most 64 fine elements, and some partition has exactly 64. `neighbour`: values below 128 are the partition's own elements, never the element itself; 128 + g is received slot g; 224 is an outflow face. Every received slot whose source partition exists is named by exactly one face of the partition.
All inputs are finite; a program needn't handle non-finite values.
Results may differ from a plain program's by a relative error of at most 0.0003.
Values sent between devices are 32-bit elements; how exact they have to be, the bound alone decides.
No kernel may reach another device: no remote copies, remote signals or barrier semaphores. Data moves between devices by JAX's collectives and lax.ppermute only.
A program may use at most 64 MiB of HBM per device.

v0:
```python
import math

import jax
import jax.numpy as jnp
from jax import lax
from jax.sharding import PartitionSpec as P

ORDER = 6


HIGH = lax.Precision.HIGHEST


def from_behind(block, axis, distance):
    devices = range(lax.axis_size(axis))
    route = [(i - distance, i) for i in devices if i - distance in devices]
    return lax.ppermute(block, axis, route)


def mix_fields(data, mats):
    return jnp.sum(data[:, :, None, :] * mats[None], axis=1)


def star_of(inv_jacobian, jacobians, material):
    nmat = jacobians.shape[0]
    fields = jacobians.shape[2]
    picked = (material[None, :] == jnp.arange(nmat, dtype=jnp.int32)[:, None]).astype(jnp.float32)
    table = jnp.transpose(jacobians.reshape(nmat, 3 * fields * fields))
    per_elem = jnp.dot(table, picked, precision=HIGH).reshape(3, fields, fields, material.shape[0])
    stacked = []
    for dim_d in range(3):
        summed = inv_jacobian[0, dim_d][None, None, :] * per_elem[0]
        for dim_c in range(1, 3):
            summed = summed + inv_jacobian[dim_c, dim_d][None, None, :] * per_elem[dim_c]
        stacked.append(summed)
    return jnp.stack(stacked)


def derivative(state, stiffness, star_mats):
    total = None
    for dim_d in range(3):
        moved = jnp.einsum("xb,xqe->bqe", stiffness[dim_d], state, precision=HIGH)
        term = mix_fields(moved, star_mats[dim_d])
        total = term if total is None else total + term
    return -total


def taylor(state, stiffness, star_mats):
    series = [state]
    for order in range(ORDER - 1):
        series.append(derivative(series[-1], stiffness, star_mats))
    return series


def integral(series, start_time, end_time):
    summed = jnp.zeros_like(series[0])
    for order in range(len(series)):
        factor = (end_time ** (order + 1) - start_time ** (order + 1)) / math.factorial(order + 1)
        summed = summed + factor * series[order]
    return summed


def volume(own_integral, stiffness, star_mats):
    total = None
    for dim_d in range(3):
        weighted = mix_fields(own_integral, star_mats[dim_d])
        term = jnp.einsum("bx,xpe->bpe", stiffness[dim_d], weighted, precision=HIGH)
        total = term if total is None else total + term
    return total


def lift_faces(solved_list, face_lift):
    faces, basis, face_basis = face_lift.shape
    lifter = jnp.transpose(face_lift, (1, 0, 2)).reshape(basis, faces * face_basis)
    return jnp.einsum("bg,gpe->bpe", lifter, jnp.concatenate(solved_list, axis=0), precision=HIGH)


def local_faces(own_integral, face_proj, face_lift, flux_own):
    faces, face_basis, basis = face_proj.shape
    projected = jnp.einsum(
        "gx,xqe->gqe", face_proj.reshape(faces * face_basis, basis), own_integral, precision=HIGH
    )
    solved_list = [
        mix_fields(projected[i * face_basis : (i + 1) * face_basis], flux_own[i])
        for i in range(faces)
    ]
    return lift_faces(solved_list, face_lift)


def neighbour_faces(
    near_list, across_face, rotation, face_proj, face_lift, face_rotate, flux_across
):
    faces, face_basis, basis = face_proj.shape
    combos = jnp.einsum("hfg,jgx->hjfx", face_rotate, face_proj, precision=HIGH).reshape(
        12 * face_basis, basis
    )
    solved_list = []
    for i in range(faces):
        near = near_list[i]
        projected = jnp.einsum("gx,xqe->gqe", combos, near, precision=HIGH)
        projected = projected.reshape(12, face_basis, near.shape[1], near.shape[2])
        choice_key = rotation[i] * 4 + across_face[i]
        pick = (choice_key[None, :] == jnp.arange(12, dtype=jnp.int32)[:, None]).astype(jnp.float32)
        chosen = jnp.sum(projected * pick[:, None, None, :], axis=0)
        solved_list.append(mix_fields(chosen, flux_across[i]))
    return lift_faces(solved_list, face_lift)


def update(
    base_state,
    own_integral,
    near_list,
    stiffness,
    star_mats,
    face_proj,
    face_lift,
    face_rotate,
    flux_own,
    flux_across,
    across_face,
    rotation,
):
    result = base_state + volume(own_integral, stiffness, star_mats)
    result = result - local_faces(own_integral, face_proj, face_lift, flux_own)
    return result - neighbour_faces(
        near_list, across_face, rotation, face_proj, face_lift, face_rotate, flux_across
    )


def route_blocks(payload, send_list):
    basis_count, field_count = (payload.shape[0], payload.shape[1])
    sub_count = lax.axis_size("sub")
    peer_count = 3 * sub_count
    block_rows = send_list.shape[0] // peer_count
    block_width = basis_count * field_count * block_rows
    outgoing = jnp.take(payload, send_list, axis=2).reshape(
        basis_count, field_count, peer_count, block_rows
    )
    out_blocks = jnp.transpose(outgoing, (2, 0, 1, 3)).reshape(peer_count, block_width)
    slab_index = lax.axis_index("dom")
    part_index = lax.axis_index("sub")
    my_part = slab_index * sub_count + part_index
    offsets = []
    for slab_hop in (-2, -1, 0, 1):
        for sub_step in range(sub_count):
            offset = slab_hop * sub_count + sub_step
            if offset != 0 and offset != -2 * sub_count:
                offsets.append(offset)
    offset_count = len(offsets)
    offset_table = jnp.array(offsets, dtype=jnp.int32)
    target = my_part + offset_table
    slab_ahead = jnp.floor_divide(target, sub_count) - slab_index
    send_ok = jnp.abs(slab_ahead) <= 1
    send_slot = jnp.where(
        send_ok, (jnp.clip(slab_ahead, -1, 1) + 1) * sub_count + jnp.remainder(target, sub_count), 0
    )
    picked_out = jnp.take(out_blocks, send_slot, axis=0)
    picked_out = jnp.where(send_ok[:, None], picked_out, 0.0)
    inbound_list = []
    for position in range(offset_count):
        inbound_list.append(from_behind(picked_out[position], ("dom", "sub"), offsets[position]))
    inbound_list.append(jnp.zeros((block_width,), payload.dtype))
    inbound_stack = jnp.stack(inbound_list)
    source = my_part - offset_table
    slab_behind = jnp.floor_divide(source, sub_count) - slab_index
    recv_ok = jnp.abs(slab_behind) <= 1
    recv_slot = jnp.where(
        recv_ok,
        (jnp.clip(slab_behind, -1, 1) + 1) * sub_count + jnp.remainder(source, sub_count),
        peer_count,
    )
    matches = (recv_slot[None, :] == jnp.arange(peer_count, dtype=jnp.int32)[:, None]).astype(
        jnp.int32
    )
    feeder = jnp.sum(matches * jnp.arange(offset_count, dtype=jnp.int32)[None, :], axis=1)
    feeder = feeder + (1 - jnp.sum(matches, axis=1)) * offset_count
    received = jnp.take(inbound_stack, feeder, axis=0)
    shaped = received.reshape(peer_count, basis_count, field_count, block_rows)
    return jnp.transpose(shaped, (1, 2, 0, 3)).reshape(
        basis_count, field_count, peer_count * block_rows
    )


def local(
    dof_state,
    stiffness,
    face_proj,
    face_lift,
    face_rotate,
    jacobians,
    material,
    inv_jacobian,
    flux_own,
    flux_across,
    cluster,
    neighbour,
    across_face,
    rotation,
    send_list,
):
    star_mats = star_of(inv_jacobian, jacobians, material)
    series = taylor(dof_state, stiffness, star_mats)
    first_half = integral(series, 0.0, 1.0)
    second_half = integral(series, 1.0, 2.0)
    is_fine = cluster == 0
    zero_column = jnp.zeros(dof_state.shape[:2] + (1,), jnp.float32)
    ext_first = jnp.concatenate(
        [first_half, route_blocks(first_half, send_list), zero_column], axis=2
    )
    near_first = [jnp.take(ext_first, neighbour[i], axis=2) for i in range(4)]
    coarse_own = first_half + second_half
    stepped = update(
        dof_state,
        first_half,
        near_first,
        stiffness,
        star_mats,
        face_proj,
        face_lift,
        face_rotate,
        flux_own,
        flux_across,
        across_face,
        rotation,
    )
    second_step = integral(taylor(stepped, stiffness, star_mats), 0.0, 1.0)
    later_half = jnp.where(is_fine, second_step, second_half)
    base_state = jnp.where(is_fine, stepped, dof_state)
    own_integral = jnp.where(is_fine, second_step, coarse_own)
    ext_later = jnp.concatenate(
        [later_half, route_blocks(later_half, send_list), zero_column], axis=2
    )
    fine_mask = is_fine[None, None, :]
    near_list = []
    for i in range(4):
        near_later = jnp.take(ext_later, neighbour[i], axis=2)
        near_list.append(jnp.where(fine_mask, near_later, near_first[i] + near_later))
    return update(
        base_state,
        own_integral,
        near_list,
        stiffness,
        star_mats,
        face_proj,
        face_lift,
        face_rotate,
        flux_own,
        flux_across,
        across_face,
        rotation,
    )


def solution(mesh):
    in_specs = (
        P(None, None, ("dom", "sub")),
        P(),
        P(),
        P(),
        P(),
        P(),
        P(("dom", "sub")),
        P(None, None, ("dom", "sub")),
        P(None, None, None, ("dom", "sub")),
        P(None, None, None, ("dom", "sub")),
        P(("dom", "sub")),
        P(None, ("dom", "sub")),
        P(None, ("dom", "sub")),
        P(None, ("dom", "sub")),
        P(("dom", "sub")),
    )
    out_specs = P(None, None, ("dom", "sub"))
    return jax.shard_map(local, mesh=mesh, in_specs=in_specs, out_specs=out_specs, check_vma=False)
```

profile of v0, /device:TPU:35, one launch (start us, length us, event | category | flops | bytes accessed | tf_op | source)
XLA Modules:
  0.0 263.3 jit_solution(10476068505582618595)
XLA Ops:
  16.8 2.8 %gather_fusion = f32[96,56,9]{1,2,0:T(8,128)} fusion(f32[56,9,128]{0,1,2:T(8,128)} %copy.187, s32[1024]{0:T(1024)S(1)} %pad_clamp_fusion.6), kind=kCustom, calls=%fused_computation.clone | custom fusion | bytes 387456 | tf_op jit(solution)/shard_map/jit(_take)/gather | solution.py:136
  20.9 2.1 copy.189
  23.0 2.2 copy.190
  27.0 15.1 %collective-permute-start = (f32[4032]{0:T(1024)}, f32[4032]{0:T(1024)}, u32[]{:S(2)}, u32[]{:S(2)}) collective-permute-start(f32[4032]{0:T(1024)} %bitcast.53), channel_id=1, source_target_pairs={{7,0},{8,1},{9,2},{10,3},{11,4},{12,5},{13,6},{14,7},{15,8},{16,9}... | collective-permute-start | bytes 48392 | tf_op jit(solution)/shard_map/ppermute | solution.py:17
  42.1 3.3 %collective-permute-start.1 = (f32[4032]{0:T(1024)}, f32[4032]{0:T(1024)}, u32[]{:S(2)}, u32[]{:S(2)}) collective-permute-start(f32[4032]{0:T(1024)} %bitcast.55), channel_id=1, source_target_pairs={{6,0},{7,1},{8,2},{9,3},{10,4},{11,5},{12,6},{13,7},{14,8},{15,9},... | collective-permute-start | bytes 48392 | tf_op jit(solution)/shard_map/ppermute | solution.py:17
  45.4 4.3 %collective-permute-start.2 = (f32[4032]{0:T(1024)}, f32[4032]{0:T(1024)}, u32[]{:S(2)}, u32[]{:S(2)}) collective-permute-start(f32[4032]{0:T(1024)} %bitcast.57), channel_id=1, source_target_pairs={{5,0},{6,1},{7,2},{8,3},{9,4},{10,5},{11,6},{12,7},{13,8},{14,9},{... | collective-permute-start | bytes 48392 | tf_op jit(solution)/shard_map/ppermute | solution.py:17
  51.7 13.6 %collective-permute-start.4 = (f32[4032]{0:T(1024)}, f32[4032]{0:T(1024)}, u32[]{:S(2)}, u32[]{:S(2)}) collective-permute-start(f32[4032]{0:T(1024)} %bitcast.61), channel_id=1, source_target_pairs={{3,0},{4,1},{5,2},{6,3},{7,4},{8,5},{9,6},{10,7},{11,8},{12,9},{13... | collective-permute-start | bytes 48392 | tf_op jit(solution)/shard_map/ppermute | solution.py:17
  84.1 5.4 %collective-permute-start.5 = (f32[4032]{0:T(1024)S(1)}, f32[4032]{0:T(1024)S(1)}, u32[]{:S(2)}, u32[]{:S(2)}) collective-permute-start(f32[4032]{0:T(1024)S(1)} %bitcast.537), channel_id=1, source_target_pairs={{2,0},{3,1},{4,2},{5,3},{6,4},{7,5},{8,6},{9,7},{10,8},{11,9},{12,... | collective-permute-start | bytes 48392 | tf_op jit(solution)/shard_map/ppermute | solution.py:17
  91.4 3.4 %collective-permute-start.7 = (f32[4032]{0:T(1024)S(1)}, f32[4032]{0:T(1024)S(1)}, u32[]{:S(2)}, u32[]{:S(2)}) collective-permute-start(f32[4032]{0:T(1024)S(1)} %bitcast.535), channel_id=1, source_target_pairs={{0,1},{1,2},{2,3},{3,4},{4,5},{5,6},{6,7},{7,8},{8,9},{9,10},{10,1... | collective-permute-start | bytes 48392 | tf_op jit(solution)/shard_map/ppermute | solution.py:17
  94.8 3.8 %collective-permute-start.8 = (f32[4032]{0:T(1024)S(1)}, f32[4032]{0:T(1024)S(1)}, u32[]{:S(2)}, u32[]{:S(2)}) collective-permute-start(f32[4032]{0:T(1024)S(1)} %bitcast.534), channel_id=1, source_target_pairs={{0,2},{1,3},{2,4},{3,5},{4,6},{5,7},{6,8},{7,9},{8,10},{9,11},{10,... | collective-permute-start | bytes 48392 | tf_op jit(solution)/shard_map/ppermute | solution.py:17
  99.2 3.3 %collective-permute-start.9 = (f32[4032]{0:T(1024)S(1)}, f32[4032]{0:T(1024)S(1)}, u32[]{:S(2)}, u32[]{:S(2)}) collective-permute-start(f32[4032]{0:T(1024)S(1)} %bitcast.533), channel_id=1, source_target_pairs={{0,3},{1,4},{2,5},{3,6},{4,7},{5,8},{6,9},{7,10},{8,11},{9,12},{10... | collective-permute-start | bytes 48392 | tf_op jit(solution)/shard_map/ppermute | solution.py:17
  104.5 4.4 %collective-permute-start.11 = (f32[4032]{0:T(1024)S(1)}, f32[4032]{0:T(1024)S(1)}, u32[]{:S(2)}, u32[]{:S(2)}) collective-permute-start(f32[4032]{0:T(1024)S(1)} %bitcast.531), channel_id=1, source_target_pairs={{0,5},{1,6},{2,7},{3,8},{4,9},{5,10},{6,11},{7,12},{8,13},{9,14},{... | collective-permute-start | bytes 48392 | tf_op jit(solution)/shard_map/ppermute | solution.py:17
  108.9 5.0 %collective-permute-start.12 = (f32[4032]{0:T(1024)S(1)}, f32[4032]{0:T(1024)S(1)}, u32[]{:S(2)}, u32[]{:S(2)}) collective-permute-start(f32[4032]{0:T(1024)S(1)} %bitcast.530), channel_id=1, source_target_pairs={{0,6},{1,7},{2,8},{3,9},{4,10},{5,11},{6,12},{7,13},{8,14},{9,15},... | collective-permute-start | bytes 48392 | tf_op jit(solution)/shard_map/ppermute | solution.py:17
  119.8 2.9 %collective-permute-done.13 = f32[4032]{0:T(1024)S(1)} collective-permute-done((f32[4032]{0:T(1024)S(1)}, f32[4032]{0:T(1024)S(1)}, u32[]{:S(2)}, u32[]{:S(2)}) %collective-permute-start.13) | collective-permute-done | bytes 16160 | tf_op jit(solution)/shard_map/ppermute | solution.py:17
  125.2 2.0 copy.191
  127.1 2.3 copy.192
  129.7 2.3 copy.194
  132.0 3.1 %gather_fusion.5 = f32[128,56,9]{1,2,0:T(8,128)} fusion(f32[56,9,225]{0,1,2:T(8,128)} %copy.194, s32[1024]{0:T(1024)S(1)} %pad_clamp_fusion.1), kind=kCustom, calls=%fused_computation.8.clone | custom fusion | bytes 516608 | tf_op jit(solution)/shard_map/jit(_take)/gather | solution.py:210
  135.1 2.2 copy.201
  137.3 3.1 %gather_fusion.4 = f32[128,56,9]{1,2,0:T(8,128)} fusion(f32[56,9,225]{0,1,2:T(8,128)} %copy.194, s32[1024]{0:T(1024)S(1)} %pad_clamp_fusion.2), kind=kCustom, calls=%fused_computation.7.clone | custom fusion | bytes 516608 | tf_op jit(solution)/shard_map/jit(_take)/gather | solution.py:210
  140.5 2.2 copy.198
  142.6 3.3 %gather_fusion.3 = f32[128,56,9]{1,2,0:T(8,128)} fusion(f32[56,9,225]{0,1,2:T(8,128)} %copy.194, s32[1024]{0:T(1024)} %pad_clamp_fusion.3), kind=kCustom, calls=%fused_computation.3.clone | custom fusion | bytes 516608 | tf_op jit(solution)/shard_map/jit(_take)/gather | solution.py:210
  145.9 2.2 copy.195
  148.1 3.3 %gather_fusion.6 = f32[128,56,9]{1,2,0:T(8,128)} fusion(f32[56,9,225]{0,1,2:T(8,128)} %copy.194, s32[1024]{0:T(1024)} %pad_clamp_fusion), kind=kCustom, calls=%fused_computation.9.clone | custom fusion | bytes 516608 | tf_op jit(solution)/shard_map/jit(_take)/gather | solution.py:210
  151.4 2.2 copy.204
  153.7 2.2 fusion.2
  156.0 2.2 fusion.1
  175.1 2.1 copy.214
  177.2 2.2 copy.215
  180.6 4.7 %collective-permute-start.14 = (f32[4032]{0:T(1024)S(1)}, f32[4032]{0:T(1024)S(1)}, u32[]{:S(2)}, u32[]{:S(2)}) collective-permute-start(f32[4032]{0:T(1024)S(1)} %bitcast.569), channel_id=1, source_target_pairs={{7,0},{8,1},{9,2},{10,3},{11,4},{12,5},{13,6},{14,7},{15,8},{16,9}... | collective-permute-start | bytes 48392 | tf_op jit(solution)/shard_map/ppermute | solution.py:17
  185.4 3.3 %collective-permute-start.15 = (f32[4032]{0:T(1024)S(1)}, f32[4032]{0:T(1024)S(1)}, u32[]{:S(2)}, u32[]{:S(2)}) collective-permute-start(f32[4032]{0:T(1024)S(1)} %bitcast.566), channel_id=1, source_target_pairs={{6,0},{7,1},{8,2},{9,3},{10,4},{11,5},{12,6},{13,7},{14,8},{15,9},... | collective-permute-start | bytes 48392 | tf_op jit(solution)/shard_map/ppermute | solution.py:17
  188.6 2.6 collective-permute-start.16
  191.3 2.2 collective-permute-start.17
  193.5 3.7 %collective-permute-start.18 = (f32[4032]{0:T(1024)S(1)}, f32[4032]{0:T(1024)S(1)}, u32[]{:S(2)}, u32[]{:S(2)}) collective-permute-start(f32[4032]{0:T(1024)S(1)} %bitcast.557), channel_id=1, source_target_pairs={{3,0},{4,1},{5,2},{6,3},{7,4},{8,5},{9,6},{10,7},{11,8},{12,9},{13... | collective-permute-start | bytes 48392 | tf_op jit(solution)/shard_map/ppermute | solution.py:17
  198.8 4.5 %collective-permute-start.19 = (f32[4032]{0:T(1024)S(1)}, f32[4032]{0:T(1024)S(1)}, u32[]{:S(2)}, u32[]{:S(2)}) collective-permute-start(f32[4032]{0:T(1024)S(1)} %bitcast.554), channel_id=1, source_target_pairs={{2,0},{3,1},{4,2},{5,3},{6,4},{7,5},{8,6},{9,7},{10,8},{11,9},{12,... | collective-permute-start | bytes 48392 | tf_op jit(solution)/shard_map/ppermute | solution.py:17
  205.3 3.4 %collective-permute-start.21 = (f32[4032]{0:T(1024)S(1)}, f32[4032]{0:T(1024)S(1)}, u32[]{:S(2)}, u32[]{:S(2)}) collective-permute-start(f32[4032]{0:T(1024)S(1)} %bitcast.549), channel_id=1, source_target_pairs={{0,1},{1,2},{2,3},{3,4},{4,5},{5,6},{6,7},{7,8},{8,9},{9,10},{10,1... | collective-permute-start | bytes 48392 | tf_op jit(solution)/shard_map/ppermute | solution.py:17
  208.6 4.7 %collective-permute-start.22 = (f32[4032]{0:T(1024)S(1)}, f32[4032]{0:T(1024)S(1)}, u32[]{:S(2)}, u32[]{:S(2)}) collective-permute-start(f32[4032]{0:T(1024)S(1)} %bitcast.548), channel_id=1, source_target_pairs={{0,2},{1,3},{2,4},{3,5},{4,6},{5,7},{6,8},{7,9},{8,10},{9,11},{10,... | collective-permute-start | bytes 48392 | tf_op jit(solution)/shard_map/ppermute | solution.py:17
  213.5 2.4 collective-permute-start.23
  215.9 2.0 collective-permute-start.24
  217.9 4.0 %collective-permute-start.25 = (f32[4032]{0:T(1024)S(1)}, f32[4032]{0:T(1024)S(1)}, u32[]{:S(2)}, u32[]{:S(2)}) collective-permute-start(f32[4032]{0:T(1024)S(1)} %bitcast.543), channel_id=1, source_target_pairs={{0,5},{1,6},{2,7},{3,8},{4,9},{5,10},{6,11},{7,12},{8,13},{9,14},{... | collective-permute-start | bytes 48392 | tf_op jit(solution)/shard_map/ppermute | solution.py:17
  222.0 5.8 %collective-permute-start.26 = (f32[4032]{0:T(1024)S(1)}, f32[4032]{0:T(1024)S(1)}, u32[]{:S(2)}, u32[]{:S(2)}) collective-permute-start(f32[4032]{0:T(1024)S(1)} %bitcast.541), channel_id=1, source_target_pairs={{0,6},{1,7},{2,8},{3,9},{4,10},{5,11},{6,12},{7,13},{8,14},{9,15},... | collective-permute-start | bytes 48392 | tf_op jit(solution)/shard_map/ppermute | solution.py:17
  227.8 2.1 collective-permute-start.27
  232.2 4.4 %collective-permute-done.27 = f32[4032]{0:T(1024)S(1)} collective-permute-done((f32[4032]{0:T(1024)S(1)}, f32[4032]{0:T(1024)S(1)}, u32[]{:S(2)}, u32[]{:S(2)}) %collective-permute-start.27) | collective-permute-done | bytes 16160 | tf_op jit(solution)/shard_map/ppermute | solution.py:17
  237.8 2.0 copy.216
  239.7 2.3 copy.217
  245.3 2.0 gather_fusion.11
  251.6 2.3 fusion.4
  257.9 2.3 fusion.6
  (396 shorter events, 91.7 us)
Async XLA Ops:
  0.0 80.4 %copy-start = (f32[3,21,21]{2,1,0:T(8,128)S(1)}, f32[3,21,21]{2,1,0:T(8,128)}, u32[]{:S(2)}) copy-start(f32[3,21,21]{2,1,0:T(8,128)} %param.29) | copy-start | bytes 15880
  25.2 41.3 %copy-start.67 = (pred[14]{0:T(512)(128)(4,1)}, pred[14]{0:T(512)(128)(4,1)S(1)}, u32[]{:S(2)}) copy-start(pred[14]{0:T(512)(128)(4,1)S(1)} %get-tuple-element.30) | copy-start | bytes 46
  25.3 41.3 %copy-start.69 = (pred[14]{0:T(512)(128)(4,1)}, pred[14]{0:T(512)(128)(4,1)S(1)}, u32[]{:S(2)}) copy-start(pred[14]{0:T(512)(128)(4,1)S(1)} %get-tuple-element.32) | copy-start | bytes 46
  25.3 41.3 %copy-start.88 = (s32[14]{0:T(128)S(1)}, s32[14]{0:T(128)}, u32[]{:S(2)}) copy-start(s32[14]{0:T(128)} %constant.163) | copy-start | bytes 172
  25.3 42.0 %copy-start.73 = (s32[4,128]{1,0:T(4,128)S(1)}, s32[4,128]{1,0:T(4,128)}, u32[]{:S(2)}) copy-start(s32[4,128]{1,0:T(4,128)} %param.36) | copy-start | bytes 6148
  25.3 42.7 %copy-start.74 = (s32[4,128]{1,0:T(4,128)S(1)}, s32[4,128]{1,0:T(4,128)}, u32[]{:S(2)}) copy-start(s32[4,128]{1,0:T(4,128)} %param.37) | copy-start | bytes 6148
  25.3 42.7 %copy-start.75 = (s32[4,128]{1,0:T(4,128)S(1)}, s32[4,128]{1,0:T(4,128)}, u32[]{:S(2)}) copy-start(s32[4,128]{1,0:T(4,128)} %param.38) | copy-start | bytes 6148
  26.0 42.0 %copy-start.33 = (f32[4,9,9,128]{3,0,2,1:T(4,128)S(1)}, f32[4,9,9,128]{3,0,2,1:T(4,128)}, u32[]{:S(2)}) copy-start(f32[4,9,9,128]{3,0,2,1:T(4,128)} %param.34) | copy-start | bytes 497668
  26.0 45.0 %copy-start.32 = (f32[4,21,56]{2,0,1:T(4,128)S(1)}, f32[4,21,56]{2,0,1:T(4,128)}, u32[]{:S(2)}) copy-start(f32[4,21,56]{2,0,1:T(4,128)} %param.27) | copy-start | bytes 56452
  27.0 57.1 %collective-permute-start = (f32[4032]{0:T(1024)}, f32[4032]{0:T(1024)}, u32[]{:S(2)}, u32[]{:S(2)}) collective-permute-start(f32[4032]{0:T(1024)} %bitcast.53), channel_id=1, source_target_pairs={{7,0},{8,1},{9,2},{10,3},{11,4},{12,5},{13,6},{14,7},{15,8},{16,9}... | collective-permute-start | bytes 48392 | tf_op jit(solution)/shard_map/ppermute | solution.py:17
  42.1 47.4 %collective-permute-start.1 = (f32[4032]{0:T(1024)}, f32[4032]{0:T(1024)}, u32[]{:S(2)}, u32[]{:S(2)}) collective-permute-start(f32[4032]{0:T(1024)} %bitcast.55), channel_id=1, source_target_pairs={{6,0},{7,1},{8,2},{9,3},{10,4},{11,5},{12,6},{13,7},{14,8},{15,9},... | collective-permute-start | bytes 48392 | tf_op jit(solution)/shard_map/ppermute | solution.py:17
  45.4 46.0 %collective-permute-start.2 = (f32[4032]{0:T(1024)}, f32[4032]{0:T(1024)}, u32[]{:S(2)}, u32[]{:S(2)}) collective-permute-start(f32[4032]{0:T(1024)} %bitcast.57), channel_id=1, source_target_pairs={{5,0},{6,1},{7,2},{8,3},{9,4},{10,5},{11,6},{12,7},{13,8},{14,9},{... | collective-permute-start | bytes 48392 | tf_op jit(solution)/shard_map/ppermute | solution.py:17
  49.7 45.1 %collective-permute-start.3 = (f32[4032]{0:T(1024)}, f32[4032]{0:T(1024)}, u32[]{:S(2)}, u32[]{:S(2)}) collective-permute-start(f32[4032]{0:T(1024)} %bitcast.59), channel_id=1, source_target_pairs={{4,0},{5,1},{6,2},{7,3},{8,4},{9,5},{10,6},{11,7},{12,8},{13,9},{1... | collective-permute-start | bytes 48392 | tf_op jit(solution)/shard_map/ppermute | solution.py:17
  51.7 47.6 %collective-permute-start.4 = (f32[4032]{0:T(1024)}, f32[4032]{0:T(1024)}, u32[]{:S(2)}, u32[]{:S(2)}) collective-permute-start(f32[4032]{0:T(1024)} %bitcast.61), channel_id=1, source_target_pairs={{3,0},{4,1},{5,2},{6,3},{7,4},{8,5},{9,6},{10,7},{11,8},{12,9},{13... | collective-permute-start | bytes 48392 | tf_op jit(solution)/shard_map/ppermute | solution.py:17
  67.3 57.1 %copy-start.59 = (s32[1024]{0:T(1024)}, s32[1024]{0:T(1024)S(1)}, u32[]{:S(2)}) copy-start(s32[1024]{0:T(1024)S(1)} %pad_clamp_fusion.4) | copy-start | bytes 12292
  68.0 85.6 %copy-start.51 = (f32[12,128]{1,0:T(8,128)}, f32[12,128]{1,0:T(8,128)S(1)}, u32[]{:S(2)}) copy-start(f32[12,128]{1,0:T(8,128)S(1)} %fusion.183) | copy-start | bytes 18436
  81.5 27.4 %copy-start.43 = (f32[1,4032]{1,0:T(1,128)S(1)}, f32[1,4032]{1,0:T(1,128)}, u32[]{:S(2)}) copy-start(f32[1,4032]{1,0:T(1,128)} %get-tuple-element.57) | copy-start | bytes 48388
  81.6 32.4 %copy-start.42 = (f32[1,4032]{1,0:T(1,128)S(1)}, f32[1,4032]{1,0:T(1,128)}, u32[]{:S(2)}) copy-start(f32[1,4032]{1,0:T(1,128)} %get-tuple-element.56) | copy-start | bytes 48388
  81.6 35.6 %copy-start.37 = (f32[1,9,9,128]{3,0,2,1:T(1,128)S(1)}, f32[1,9,9,128]{3,0,2,1:T(1,128)}, u32[]{:S(2)}) copy-start(f32[1,9,9,128]{3,0,2,1:T(1,128)} %get-tuple-element.74) | copy-start | bytes 124420
  82.0 35.8 %copy-start.36 = (f32[1,9,9,128]{3,0,2,1:T(1,128)S(1)}, f32[1,9,9,128]{3,0,2,1:T(1,128)}, u32[]{:S(2)}) copy-start(f32[1,9,9,128]{3,0,2,1:T(1,128)} %get-tuple-element.75) | copy-start | bytes 124420
  82.0 36.4 %copy-start.35 = (f32[1,9,9,128]{3,0,2,1:T(1,128)S(1)}, f32[1,9,9,128]{3,0,2,1:T(1,128)}, u32[]{:S(2)}) copy-start(f32[1,9,9,128]{3,0,2,1:T(1,128)} %get-tuple-element.73) | copy-start | bytes 124420
  82.0 37.0 %copy-start.34 = (f32[1,9,9,128]{3,0,2,1:T(1,128)S(1)}, f32[1,9,9,128]{3,0,2,1:T(1,128)}, u32[]{:S(2)}) copy-start(f32[1,9,9,128]{3,0,2,1:T(1,128)} %get-tuple-element.76) | copy-start | bytes 124420
  84.0 41.0 %copy-start.65 = (pred[12]{0:T(512)(128)(4,1)S(1)}, pred[12]{0:T(512)(128)(4,1)}, u32[]{:S(2)}) copy-start(pred[12]{0:T(512)(128)(4,1)} %get-tuple-element.28) | copy-start | bytes 40
  84.0 53.3 %copy-start.60 = (s32[1024]{0:T(1024)}, s32[1024]{0:T(1024)S(1)}, u32[]{:S(2)}) copy-start(s32[1024]{0:T(1024)S(1)} %pad_clamp_fusion.2) | copy-start | bytes 12292
  84.1 18.4 %collective-permute-start.5 = (f32[4032]{0:T(1024)S(1)}, f32[4032]{0:T(1024)S(1)}, u32[]{:S(2)}, u32[]{:S(2)}) collective-permute-start(f32[4032]{0:T(1024)S(1)} %bitcast.537), channel_id=1, source_target_pairs={{2,0},{3,1},{4,2},{5,3},{6,4},{7,5},{8,6},{9,7},{10,8},{11,9},{12,... | collective-permute-start | bytes 48392 | tf_op jit(solution)/shard_map/ppermute | solution.py:17
  89.5 15.0 %collective-permute-start.6 = (f32[4032]{0:T(1024)S(1)}, f32[4032]{0:T(1024)S(1)}, u32[]{:S(2)}, u32[]{:S(2)}) collective-permute-start(f32[4032]{0:T(1024)S(1)} %bitcast.536), channel_id=1, source_target_pairs={{1,0},{2,1},{3,2},{4,3},{5,4},{6,5},{7,6},{8,7},{9,8},{10,9},{11,1... | collective-permute-start | bytes 48392 | tf_op jit(solution)/shard_map/ppermute | solution.py:17
  91.4 17.5 %collective-permute-start.7 = (f32[4032]{0:T(1024)S(1)}, f32[4032]{0:T(1024)S(1)}, u32[]{:S(2)}, u32[]{:S(2)}) collective-permute-start(f32[4032]{0:T(1024)S(1)} %bitcast.535), channel_id=1, source_target_pairs={{0,1},{1,2},{2,3},{3,4},{4,5},{5,6},{6,7},{7,8},{8,9},{9,10},{10,1... | collective-permute-start | bytes 48392 | tf_op jit(solution)/shard_map/ppermute | solution.py:17
  94.8 19.1 %collective-permute-start.8 = (f32[4032]{0:T(1024)S(1)}, f32[4032]{0:T(1024)S(1)}, u32[]{:S(2)}, u32[]{:S(2)}) collective-permute-start(f32[4032]{0:T(1024)S(1)} %bitcast.534), channel_id=1, source_target_pairs={{0,2},{1,3},{2,4},{3,5},{4,6},{5,7},{6,8},{7,9},{8,10},{9,11},{10,... | collective-permute-start | bytes 48392 | tf_op jit(solution)/shard_map/ppermute | solution.py:17
  99.2 20.5 %collective-permute-start.9 = (f32[4032]{0:T(1024)S(1)}, f32[4032]{0:T(1024)S(1)}, u32[]{:S(2)}, u32[]{:S(2)}) collective-permute-start(f32[4032]{0:T(1024)S(1)} %bitcast.533), channel_id=1, source_target_pairs={{0,3},{1,4},{2,5},{3,6},{4,7},{5,8},{6,9},{7,10},{8,11},{9,12},{10... | collective-permute-start | bytes 48392 | tf_op jit(solution)/shard_map/ppermute | solution.py:17
  102.5 17.2 %collective-permute-start.10 = (f32[4032]{0:T(1024)S(1)}, f32[4032]{0:T(1024)S(1)}, u32[]{:S(2)}, u32[]{:S(2)}) collective-permute-start(f32[4032]{0:T(1024)S(1)} %bitcast.532), channel_id=1, source_target_pairs={{0,4},{1,5},{2,6},{3,7},{4,8},{5,9},{6,10},{7,11},{8,12},{9,13},{1... | collective-permute-start | bytes 48392 | tf_op jit(solution)/shard_map/ppermute | solution.py:17
  104.5 15.3 %collective-permute-start.11 = (f32[4032]{0:T(1024)S(1)}, f32[4032]{0:T(1024)S(1)}, u32[]{:S(2)}, u32[]{:S(2)}) collective-permute-start(f32[4032]{0:T(1024)S(1)} %bitcast.531), channel_id=1, source_target_pairs={{0,5},{1,6},{2,7},{3,8},{4,9},{5,10},{6,11},{7,12},{8,13},{9,14},{... | collective-permute-start | bytes 48392 | tf_op jit(solution)/shard_map/ppermute | solution.py:17
  108.9 10.8 %collective-permute-start.12 = (f32[4032]{0:T(1024)S(1)}, f32[4032]{0:T(1024)S(1)}, u32[]{:S(2)}, u32[]{:S(2)}) collective-permute-start(f32[4032]{0:T(1024)S(1)} %bitcast.530), channel_id=1, source_target_pairs={{0,6},{1,7},{2,8},{3,9},{4,10},{5,11},{6,12},{7,13},{8,14},{9,15},... | collective-permute-start | bytes 48392 | tf_op jit(solution)/shard_map/ppermute | solution.py:17
  114.0 8.7 %collective-permute-start.13 = (f32[4032]{0:T(1024)S(1)}, f32[4032]{0:T(1024)S(1)}, u32[]{:S(2)}, u32[]{:S(2)}) collective-permute-start(f32[4032]{0:T(1024)S(1)} %bitcast.529), channel_id=1, source_target_pairs={{0,7},{1,8},{2,9},{3,10},{4,11},{5,12},{6,13},{7,14},{8,15},{9,16}... | collective-permute-start | bytes 48392 | tf_op jit(solution)/shard_map/ppermute | solution.py:17
  180.6 18.2 %collective-permute-start.14 = (f32[4032]{0:T(1024)S(1)}, f32[4032]{0:T(1024)S(1)}, u32[]{:S(2)}, u32[]{:S(2)}) collective-permute-start(f32[4032]{0:T(1024)S(1)} %bitcast.569), channel_id=1, source_target_pairs={{7,0},{8,1},{9,2},{10,3},{11,4},{12,5},{13,6},{14,7},{15,8},{16,9}... | collective-permute-start | bytes 48392 | tf_op jit(solution)/shard_map/ppermute | solution.py:17
  185.4 17.9 %collective-permute-start.15 = (f32[4032]{0:T(1024)S(1)}, f32[4032]{0:T(1024)S(1)}, u32[]{:S(2)}, u32[]{:S(2)}) collective-permute-start(f32[4032]{0:T(1024)S(1)} %bitcast.566), channel_id=1, source_target_pairs={{6,0},{7,1},{8,2},{9,3},{10,4},{11,5},{12,6},{13,7},{14,8},{15,9},... | collective-permute-start | bytes 48392 | tf_op jit(solution)/shard_map/ppermute | solution.py:17
  188.6 16.6 %collective-permute-start.16 = (f32[4032]{0:T(1024)S(1)}, f32[4032]{0:T(1024)S(1)}, u32[]{:S(2)}, u32[]{:S(2)}) collective-permute-start(f32[4032]{0:T(1024)S(1)} %bitcast.563), channel_id=1, source_target_pairs={{5,0},{6,1},{7,2},{8,3},{9,4},{10,5},{11,6},{12,7},{13,8},{14,9},{... | collective-permute-start | bytes 48392 | tf_op jit(solution)/shard_map/ppermute | solution.py:17
  191.3 17.4 %collective-permute-start.17 = (f32[4032]{0:T(1024)S(1)}, f32[4032]{0:T(1024)S(1)}, u32[]{:S(2)}, u32[]{:S(2)}) collective-permute-start(f32[4032]{0:T(1024)S(1)} %bitcast.560), channel_id=1, source_target_pairs={{4,0},{5,1},{6,2},{7,3},{8,4},{9,5},{10,6},{11,7},{12,8},{13,9},{1... | collective-permute-start | bytes 48392 | tf_op jit(solution)/shard_map/ppermute | solution.py:17
  193.5 20.0 %collective-permute-start.18 = (f32[4032]{0:T(1024)S(1)}, f32[4032]{0:T(1024)S(1)}, u32[]{:S(2)}, u32[]{:S(2)}) collective-permute-start(f32[4032]{0:T(1024)S(1)} %bitcast.557), channel_id=1, source_target_pairs={{3,0},{4,1},{5,2},{6,3},{7,4},{8,5},{9,6},{10,7},{11,8},{12,9},{13... | collective-permute-start | bytes 48392 | tf_op jit(solution)/shard_map/ppermute | solution.py:17
  197.8 38.8 %copy-start.39 = (f32[1,4032]{1,0:T(1,128)S(1)}, f32[1,4032]{1,0:T(1,128)}, u32[]{:S(2)}) copy-start(f32[1,4032]{1,0:T(1,128)} %copy-done.38) | copy-start | bytes 48388
  198.8 17.1 %collective-permute-start.19 = (f32[4032]{0:T(1024)S(1)}, f32[4032]{0:T(1024)S(1)}, u32[]{:S(2)}, u32[]{:S(2)}) collective-permute-start(f32[4032]{0:T(1024)S(1)} %bitcast.554), channel_id=1, source_target_pairs={{2,0},{3,1},{4,2},{5,3},{6,4},{7,5},{8,6},{9,7},{10,8},{11,9},{12,... | collective-permute-start | bytes 48392 | tf_op jit(solution)/shard_map/ppermute | solution.py:17
  203.3 14.6 %collective-permute-start.20 = (f32[4032]{0:T(1024)S(1)}, f32[4032]{0:T(1024)S(1)}, u32[]{:S(2)}, u32[]{:S(2)}) collective-permute-start(f32[4032]{0:T(1024)S(1)} %bitcast.551), channel_id=1, source_target_pairs={{1,0},{2,1},{3,2},{4,3},{5,4},{6,5},{7,6},{8,7},{9,8},{10,9},{11,1... | collective-permute-start | bytes 48392 | tf_op jit(solution)/shard_map/ppermute | solution.py:17
  205.3 16.7 %collective-permute-start.21 = (f32[4032]{0:T(1024)S(1)}, f32[4032]{0:T(1024)S(1)}, u32[]{:S(2)}, u32[]{:S(2)}) collective-permute-start(f32[4032]{0:T(1024)S(1)} %bitcast.549), channel_id=1, source_target_pairs={{0,1},{1,2},{2,3},{3,4},{4,5},{5,6},{6,7},{7,8},{8,9},{9,10},{10,1... | collective-permute-start | bytes 48392 | tf_op jit(solution)/shard_map/ppermute | solution.py:17
  208.6 19.2 %collective-permute-start.22 = (f32[4032]{0:T(1024)S(1)}, f32[4032]{0:T(1024)S(1)}, u32[]{:S(2)}, u32[]{:S(2)}) collective-permute-start(f32[4032]{0:T(1024)S(1)} %bitcast.548), channel_id=1, source_target_pairs={{0,2},{1,3},{2,4},{3,5},{4,6},{5,7},{6,8},{7,9},{8,10},{9,11},{10,... | collective-permute-start | bytes 48392 | tf_op jit(solution)/shard_map/ppermute | solution.py:17
  213.5 16.9 %collective-permute-start.23 = (f32[4032]{0:T(1024)S(1)}, f32[4032]{0:T(1024)S(1)}, u32[]{:S(2)}, u32[]{:S(2)}) collective-permute-start(f32[4032]{0:T(1024)S(1)} %bitcast.547), channel_id=1, source_target_pairs={{0,3},{1,4},{2,5},{3,6},{4,7},{5,8},{6,9},{7,10},{8,11},{9,12},{10... | collective-permute-start | bytes 48392 | tf_op jit(solution)/shard_map/ppermute | solution.py:17
  215.9 14.5 %collective-permute-start.24 = (f32[4032]{0:T(1024)S(1)}, f32[4032]{0:T(1024)S(1)}, u32[]{:S(2)}, u32[]{:S(2)}) collective-permute-start(f32[4032]{0:T(1024)S(1)} %bitcast.545), channel_id=1, source_target_pairs={{0,4},{1,5},{2,6},{3,7},{4,8},{5,9},{6,10},{7,11},{8,12},{9,13},{1... | collective-permute-start | bytes 48392 | tf_op jit(solution)/shard_map/ppermute | solution.py:17
  217.9 12.5 %collective-permute-start.25 = (f32[4032]{0:T(1024)S(1)}, f32[4032]{0:T(1024)S(1)}, u32[]{:S(2)}, u32[]{:S(2)}) collective-permute-start(f32[4032]{0:T(1024)S(1)} %bitcast.543), channel_id=1, source_target_pairs={{0,5},{1,6},{2,7},{3,8},{4,9},{5,10},{6,11},{7,12},{8,13},{9,14},{... | collective-permute-start | bytes 48392 | tf_op jit(solution)/shard_map/ppermute | solution.py:17
  222.0 10.2 %collective-permute-start.26 = (f32[4032]{0:T(1024)S(1)}, f32[4032]{0:T(1024)S(1)}, u32[]{:S(2)}, u32[]{:S(2)}) collective-permute-start(f32[4032]{0:T(1024)S(1)} %bitcast.541), channel_id=1, source_target_pairs={{0,6},{1,7},{2,8},{3,9},{4,10},{5,11},{6,12},{7,13},{8,14},{9,15},... | collective-permute-start | bytes 48392 | tf_op jit(solution)/shard_map/ppermute | solution.py:17
  227.8 8.7 %collective-permute-start.27 = (f32[4032]{0:T(1024)S(1)}, f32[4032]{0:T(1024)S(1)}, u32[]{:S(2)}, u32[]{:S(2)}) collective-permute-start(f32[4032]{0:T(1024)S(1)} %bitcast.539), channel_id=1, source_target_pairs={{0,7},{1,8},{2,9},{3,10},{4,11},{5,12},{6,13},{7,14},{8,15},{9,16}... | collective-permute-start | bytes 48392 | tf_op jit(solution)/shard_map/ppermute | solution.py:17
  (71 other events, 538.8 us)
where the time goes:
time: 267 us; the launch traced here: 263 us
  starting transfers between devices  117 us (44%)
  local copies, waits for them, and re-layouts  79.9 us (30%)
  matrix products  38.1 us (14%)
  other arithmetic  17.1 us (6%)
  waiting for transfers between devices  9.06 us (3%)
    ppermute x28, starting transfers between devices, from_behind(): return lax.ppermute(block, axis, route)  117 us
    gather x8, local copies, waits for them, and re-layouts, local(): near_first = [jnp.take(ext_first, neighbour[i], axis=2) for i in range(4)]  21.6 us
    dot_general x30, matrix products, derivative(): moved = jnp.einsum('xb,xqe->bqe', stiffness[dim_d], state, precision=HIGH)  16.3 us
    dot_general x8, matrix products, neighbour_faces(): projected = jnp.einsum('gx,xqe->gqe', combos, near, precision=HIGH)  13.8 us
    gather x8, local copies, waits for them, and re-layouts, local(): near_later = jnp.take(ext_later, neighbour[i], axis=2)  10.8 us
    reduce_sum x47, other arithmetic, mix_fields(): return jnp.sum(data[:, :, None, :] * mats[None], axis=1)  9.2 us
    ppermute x28, waiting for transfers between devices, from_behind(): return lax.ppermute(block, axis, route)  9.06 us
    unnamed x192, local copies, waits for them, and re-layouts  8.16 us
  transfers between devices with their start and end apart: 28, of which 3 were waited for; matrix products, arithmetic and copies ran while one was open for 9% of the time, Pallas kernels for 0%

commit v1 on v0

v1 whole, which is shorter than its diff:
```python
import math

import jax
import jax.numpy as jnp
from jax import lax
from jax.experimental import pallas as pl
from jax.experimental.pallas import tpu as pltpu
from jax.sharding import PartitionSpec as P

ORDER = 6
NB, NF, FB, EL = 56, 9, 21, 128
FP = 24
WID = NF * EL
HIGH = lax.Precision.HIGHEST
F32 = jnp.float32
BF16 = jnp.bfloat16
AXES = ("dom", "sub")


def dot32(a, b):
    return jnp.dot(a, b, preferred_element_type=F32)


def halves(x):
    hi = x.astype(BF16)
    return hi, (x - hi.astype(F32)).astype(BF16)


def put_rhs(rhs, cols, x):
    hi, lo = halves(jnp.concatenate([x, jnp.zeros((8, x.shape[1]), F32)], axis=0))
    rhs[0:64, cols] = hi
    rhs[64:128, cols] = lo
    rhs[128:192, cols] = hi


def put_lhs(lhs, rows, a):
    hi, lo = halves(a)
    lhs[rows, 0:NB] = hi
    lhs[rows, 64 : 64 + NB] = hi
    lhs[rows, 128 : 128 + NB] = lo


def field(p):
    return slice(p * EL, (p + 1) * EL)


PAIRS = ((0, 1), (2, 3), (4, 5), (6, 7), (8,))


def pair_cols(group):
    return slice(group[0] * EL, (group[-1] + 1) * EL)


def mix_star(moved, star, group):
    acc = [None] * len(group)
    for d in range(3):
        for q in range(NF):
            m = moved[d * NB : (d + 1) * NB, field(q)].reshape(7, 8, EL)
            for n, p in enumerate(group):
                t = m * star[pl.ds(d * 81 + q * 9 + p, 8, stride=0), :][None]
                acc[n] = t if acc[n] is None else acc[n] + t
    return [a.reshape(NB, EL) for a in acc]


def run_series(lhs, rhs, moved, star, add):
    for group in PAIRS:
        cols = pair_cols(group)
        moved[0, :, cols] = dot32(lhs[...], rhs[:, cols])
    for order in range(1, ORDER):
        src = moved.at[(order - 1) % 2]
        for group in PAIRS:
            cols = pair_cols(group)
            for p, block in zip(group, mix_star(src, star, group)):
                add(order, p, block)
                if order < ORDER - 1:
                    put_rhs(rhs, field(p), block)
            if order < ORDER - 1:
                moved[order % 2, :, cols] = dot32(lhs[...], rhs[:, cols])


def pack_blocks(ids, send, payload, gat, res, trans, other, main):
    slots = jnp.concatenate([send[...], jnp.full((1, EL - send.shape[1]), -1, jnp.int32)], axis=1)
    rows = lax.broadcasted_iota(jnp.int32, (EL, EL), 0)
    pick = jnp.where(rows == slots, 1.0, 0.0).astype(BF16)
    pick = jnp.concatenate([pick, pick], axis=0)
    for q in range(NF):
        x = jnp.concatenate([payload[:, field(q)], jnp.zeros((8, EL), F32)], axis=0)
        hi, lo = halves(x)
        gat[q * 64 : (q + 1) * 64, 0:EL] = hi
        gat[q * 64 : (q + 1) * 64, EL : 2 * EL] = lo
    got = dot32(gat[...], pick)
    for q in range(NF):
        res[q * NB : (q + 1) * NB, :] = got[q * 64 : q * 64 + NB]
    res[NF * NB : 512, :] = jnp.zeros((8, EL), F32)
    trans[...] = res[...].T
    core = ids[0]
    for r in range(4):
        other[r] = trans[pl.ds(pl.multiple_of(8 * (2 * core * 4 + r), 8), 8), :]
    for c in range(2):
        for r in range(4):
            main[c * 4 + r] = trans[pl.ds(pl.multiple_of(8 * ((c - core + 1) * 4 + r), 8), 8), :]


def k_predict(ids, dof, stiff, jac, mat, inv, send, star, first, second, other, main, lhs_out, lhs, rhs, moved, gat, res, trans):
    pick = (lax.broadcasted_iota(jnp.int32, (16, EL), 0) == mat[...]).astype(F32)
    per = [jnp.dot(jac[:, c, :], pick, precision=HIGH, preferred_element_type=F32) for c in range(3)]
    for d in range(3):
        total = None
        for c in range(3):
            t = per[c] * inv[c, pl.ds(d, 1), :]
            total = t if total is None else total + t
        star[d * 81 : (d + 1) * 81, :] = total
    lhs[...] = jnp.zeros(lhs.shape, BF16)
    for d in range(3):
        put_lhs(lhs, slice(d * NB, (d + 1) * NB), -(stiff[d].T))
    lhs_out[...] = lhs[...]
    for p in range(NF):
        x = dof[p]
        put_rhs(rhs, field(p), x)
        first[:, field(p)] = x
        second[:, field(p)] = x

    def add(order, p, block):
        scale = 1.0 / math.factorial(order + 1)
        first[:, field(p)] = first[:, field(p)] + scale * block
        second[:, field(p)] = second[:, field(p)] + ((2 ** (order + 1) - 1) * scale) * block

    run_series(lhs, rhs, moved, star, add)
    pack_blocks(ids, send, first, gat, res, trans, other, main)


def face_mix(source, flux, face, p, lane):
    acc = None
    for q in range(NF):
        t = source(q).reshape(3, 8, EL) * jnp.broadcast_to(flux[q * 9 + p, pl.ds(face, 1), :], (8, EL))[None]
        acc = t if acc is None else acc + t
    return acc.reshape(FP, EL)


def own_terms(both, rhs, moved, star, flux_own, lift_own, solved, put):
    for group in PAIRS:
        cols = pair_cols(group)
        moved[:, cols] = dot32(both[...], rhs[:, cols])
    for p in range(NF):
        for i in range(4):
            base = 3 * NB + i * FP
            s = face_mix(lambda q: moved[base : base + FP, field(q)], flux_own, i, p, EL)
            solved[i * FP : (i + 1) * FP, field(p)] = s
    for group in PAIRS:
        cols = pair_cols(group)
        hi, lo = halves(solved[:, cols])
        lifted = dot32(lift_own[0], hi) + dot32(lift_own[0], lo) + dot32(lift_own[1], hi)
        for n, (p, block) in enumerate(zip(group, mix_star(moved, star, group))):
            put(p, block + lifted[:, n * EL : (n + 1) * EL])


def gather_table(source, table):
    for q in range(NF):
        for j in range(4):
            table[q * FP : (q + 1) * FP, j * EL : (j + 1) * EL] = source(j, q)
    table[NF * FP : 224, :] = jnp.zeros((8, 4 * EL), F32)


def gather_from(table, hot):
    hi, lo = halves(table[...])
    return dot32(hi, hot) + dot32(lo, hot)


def k_window_a(first, dof, star, stiff, proj, lift, rotate, flux_own, nbr, across,
               base, chosen, hot_own, hot_ghost, both, lift_own, lift_rot,
               rhs, moved, solved, table, lift_f, rot_f):
    both[...] = jnp.zeros(both.shape, BF16)
    for d in range(3):
        put_lhs(both, slice(d * NB, (d + 1) * NB), stiff[d])
    for j in range(4):
        a = jnp.concatenate([proj[:, j, :], jnp.zeros((3, NB), F32)], axis=0)
        put_lhs(both, slice(3 * NB + j * FP, 3 * NB + (j + 1) * FP), a)
    lift_f[...] = jnp.zeros(lift_f.shape, F32)
    rot_f[...] = jnp.zeros(rot_f.shape, F32)
    for i in range(4):
        a = -lift[:, i, :]
        lift_f[i * FP : i * FP + FB, :] = a
        for h in range(3):
            turned = lax.dot_general(rotate[h], a, (((0,), (0,)), ((), ())), precision=HIGH, preferred_element_type=F32)
            rot_f[h * 96 + i * FP : h * 96 + i * FP + FB, :] = turned
    lo_hi, lo_lo = halves(lift_f[...].T)
    lift_own[0] = lo_hi
    lift_own[1] = lo_lo
    lr_hi, lr_lo = halves(rot_f[...].T)
    lift_rot[0:NB] = lr_hi
    lift_rot[NB : 2 * NB] = lr_lo
    rows = lax.broadcasted_iota(jnp.int32, (EL, EL), 0)
    for i in range(4):
        n = nbr[pl.ds(i, 1), :]
        key = across[pl.ds(i, 1), :] * EL + jnp.where(n < EL, n, n + (3 * EL))
        for j in range(4):
            hot_own[j * EL : (j + 1) * EL, field(i)] = jnp.where(rows + j * EL == key, 1.0, 0.0).astype(BF16)
            hot_ghost[j * EL : (j + 1) * EL, field(i)] = jnp.where(rows + (j + 4) * EL == key, 1.0, 0.0).astype(BF16)
    for p in range(NF):
        put_rhs(rhs, field(p), first[:, field(p)])

    def put(p, block):
        base[:, field(p)] = dof[p] + block

    own_terms(both, rhs, moved, star, flux_own, lift_own, solved, put)
    gather_table(lambda j, q: moved[3 * NB + j * FP : 3 * NB + (j + 1) * FP, field(q)], table)
    chosen[...] = gather_from(table, hot_own[...])


def k_window_b(later, own, part, star, flux_own, hot_own, both, lift_own,
               base, chosen, rhs, moved, solved, table, proj_b):
    for p in range(NF):
        put_rhs(rhs, field(p), later[:, field(p)])
    for group in PAIRS:
        cols = pair_cols(group)
        proj_b[:, cols] = dot32(both[3 * NB :, :], rhs[:, cols])
    gather_table(lambda j, q: proj_b[j * FP : (j + 1) * FP, field(q)], table)
    chosen[...] = gather_from(table, hot_own[...])
    for p in range(NF):
        put_rhs(rhs, field(p), own[:, field(p)])

    def put(p, block):
        base[:, field(p)] = part[:, field(p)] + block

    own_terms(both, rhs, moved, star, flux_own, lift_own, solved, put)


def near_terms(ids, recv, chosen, hot_ghost, both, lift_rot, flux_across, rot,
               ghost, ghost_t, rhs, proj_g, table, near, solved, turned, put):
    core = ids[0]
    pos = ids[1]
    for s in range(4):
        keep = jnp.where(pos == s, 0.0, 1.0).astype(F32)
        ghost[(4 + s) * 8 : (5 + s) * 8, :] = recv[0, core * 4 + s] * keep
        row = pl.multiple_of(8 * ((2 - 2 * core) * 4 + s), 8)
        ghost[pl.ds(row, 8), :] = recv[0, (1 - core) * 4 + s]
        row = pl.multiple_of(8 * (2 * core * 4 + s), 8)
        ghost[pl.ds(row, 8), :] = recv[1, core * 4 + s]
    ghost[96:EL, :] = jnp.zeros((EL - 96, 512), F32)
    ghost_t[...] = ghost[...].T
    for q in range(NF):
        put_rhs(rhs, field(q), ghost_t[q * NB : (q + 1) * NB, :])
    for group in PAIRS:
        cols = pair_cols(group)
        proj_g[:, cols] = dot32(both[3 * NB :, :], rhs[:, cols])
    gather_table(lambda j, q: proj_g[j * FP : (j + 1) * FP, field(q)], table)
    near[...] = chosen[...] + gather_from(table, hot_ghost[...])
    for p in range(NF):
        for i in range(4):
            s = face_mix(lambda q: near[q * FP : (q + 1) * FP, field(i)], flux_across, i, p, EL)
            solved[i * FP : (i + 1) * FP, field(p)] = s
    masks = []
    for h in range(3):
        m = [jnp.broadcast_to(jnp.where(rot[pl.ds(i, 1), :] == h, 1.0, 0.0), (FP, EL)) for i in range(4)]
        masks.append(jnp.concatenate(m, axis=0).astype(BF16))
    for group in PAIRS:
        for p in group:
            hi, lo = halves(solved[:, field(p)])
            for h in range(3):
                turned[0, h * 96 : (h + 1) * 96, field(p)] = hi * masks[h]
                turned[1, h * 96 : (h + 1) * 96, field(p)] = lo * masks[h]
        cols = pair_cols(group)
        top = dot32(lift_rot[...], turned[0, :, cols])
        put(group, top[0:NB] + top[NB : 2 * NB] + dot32(lift_rot[0:NB, :], turned[1, :, cols]))


def k_middle(ids, recv, chosen, hot_ghost, both, lift_rot, flux_across, rot, base, lhs, star, first, second, dof, cluster, send,
             later, own, part, other, main,
             ghost, ghost_t, rhs, proj_g, table, near, solved, turned, moved, total, gat, res):
    fine = cluster[...] == 0

    def put(group, block):
        for n, p in enumerate(group):
            b = block[:, n * EL : (n + 1) * EL]
            stepped = base[:, field(p)] + b
            part[:, field(p)] = jnp.where(fine, stepped, dof[p] + b)
            total[:, field(p)] = stepped
            put_rhs(rhs, field(p), stepped)

    near_terms(ids, recv, chosen, hot_ghost, both, lift_rot, flux_across, rot,
               ghost, ghost_t, rhs, proj_g, table, near, solved, turned, put)

    def add(order, p, block):
        scale = 1.0 / math.factorial(order + 1)
        t = total[:, field(p)] + scale * block
        if order < ORDER - 1:
            total[:, field(p)] = t
        else:
            sec = second[:, field(p)]
            later[:, field(p)] = jnp.where(fine, t, sec)
            own[:, field(p)] = jnp.where(fine, t, first[:, field(p)] + sec)

    run_series(lhs, rhs, moved, star, add)
    pack_blocks(ids, send, later, gat, res, ghost, other, main)


def k_final(ids, recv, chosen, hot_ghost, both, lift_rot, flux_across, rot, base, out,
            ghost, ghost_t, rhs, proj_g, table, near, solved, turned):
    def put(group, block):
        for n, p in enumerate(group):
            out[p] = base[:, field(p)] + block[:, n * EL : (n + 1) * EL]

    near_terms(ids, recv, chosen, hot_ghost, both, lift_rot, flux_across, rot,
               ghost, ghost_t, rhs, proj_g, table, near, solved, turned, put)


def call(kernel, name, outs, scratch, smem_first, *args):
    space = [pl.BlockSpec(memory_space=pltpu.VMEM) for _ in args]
    if smem_first:
        space[0] = pl.BlockSpec(memory_space=pltpu.SMEM)
    return pl.pallas_call(
        kernel,
        out_shape=[jax.ShapeDtypeStruct(s, d) for s, d in outs],
        in_specs=space,
        out_specs=[pl.BlockSpec(memory_space=pltpu.VMEM) for _ in outs],
        scratch_shapes=[pltpu.VMEM(s, d) for s, d in scratch],
        name=name,
    )(*args)


def exchange_start(other, slabs):
    pairs = []
    for a in range(1, slabs - 1, 2):
        for s in range(4):
            pairs += [(a * 4 + s, (a + 1) * 4 + s), ((a + 1) * 4 + s, a * 4 + s)]
    return lax.ppermute(other, AXES, pairs)


def exchange_end(relay, main, slabs):
    groups = [[(2 * c + b) * 4 + s for b in range(2) for s in range(4)] for c in range(slabs // 2)]
    message = jnp.stack([main, jnp.concatenate([relay, relay], axis=0)])
    return lax.all_to_all(message, AXES, 1, 1, axis_index_groups=groups)


def local(dof_state, stiffness, face_proj, face_lift, face_rotate, jacobians, material, inv_jacobian,
          flux_own, flux_across, cluster, neighbour, across_face, rotation, send_list):
    slabs = lax.axis_size("dom")
    ids = jnp.stack([lax.axis_index("dom") % 2, lax.axis_index("sub")]).astype(jnp.int32)
    dof = jnp.transpose(dof_state, (1, 0, 2))
    jac = jnp.transpose(jacobians, (2, 3, 1, 0)).reshape(81, 3, 16)
    proj = jnp.transpose(face_proj, (1, 0, 2))
    lift = jnp.transpose(face_lift, (2, 0, 1))
    f_own = jnp.transpose(flux_own, (1, 2, 0, 3)).reshape(81, 4, EL)
    f_across = jnp.transpose(flux_across, (1, 2, 0, 3)).reshape(81, 4, EL)
    mat = material.reshape(1, EL)
    clu = cluster.reshape(1, EL)
    send = send_list.reshape(1, 96)
    state = ((NB, WID), F32)
    blocks = [((4, 8, 512), F32), ((8, 8, 512), F32)]
    rhs = ((192, WID), BF16)
    pack = [((576, 2 * EL), BF16), ((512, EL), F32), ((EL, 512), F32)]
    star, first, second, other, main, lhs = call(
        k_predict, "predict", [((243, EL), F32), state, state, *blocks, ((168, 192), BF16)],
        [((168, 192), BF16), rhs, ((2, 168, WID), F32), *pack],
        True, ids, dof, stiffness, jac, mat, inv_jacobian, send)
    relay = exchange_start(other, slabs)
    table = ((224, 512), F32)
    hot = ((512, 512), BF16)
    base, chosen, hot_own, hot_ghost, both, lift_own, lift_rot = call(
        k_window_a, "window_a",
        [state, table, hot, hot, ((264, 192), BF16), ((2, NB, 96), BF16), ((2 * NB, 288), BF16)],
        [rhs, ((264, WID), F32), ((96, WID), F32), table, ((96, NB), F32), ((288, NB), F32)],
        False, first, dof, star, stiffness, proj, lift, face_rotate, f_own, neighbour, across_face)
    recv = exchange_end(relay, main, slabs)
    near_scratch = [((EL, 512), F32), ((512, EL), F32), rhs, ((96, WID), F32), table, table, ((96, WID), F32), ((2, 288, WID), BF16)]
    later, own, part, other, main = call(
        k_middle, "middle", [state, state, state, *blocks],
        [*near_scratch, ((2, 168, WID), F32), state, pack[0], pack[1]],
        True, ids, recv, chosen, hot_ghost, both, lift_rot, f_across, rotation, base, lhs, star, first, second, dof, clu, send)
    relay = exchange_start(other, slabs)
    base, chosen = call(
        k_window_b, "window_b", [state, table],
        [rhs, ((264, WID), F32), ((96, WID), F32), table, ((96, WID), F32)],
        False, later, own, part, star, f_own, hot_own, both, lift_own)
    recv = exchange_end(relay, main, slabs)
    (out,) = call(
        k_final, "final", [((NF, NB, EL), F32)], near_scratch,
        True, ids, recv, chosen, hot_ghost, both, lift_rot, f_across, rotation, base)
    return jnp.transpose(out, (1, 0, 2))


def solution(mesh):
    both = ("dom", "sub")
    in_specs = (
        P(None, None, both), P(), P(), P(), P(), P(), P(both), P(None, None, both),
        P(None, None, None, both), P(None, None, None, both), P(both), P(None, both),
        P(None, both), P(None, both), P(both),
    )
    return jax.shard_map(local, mesh=mesh, in_specs=in_specs, out_specs=P(None, None, both), check_vma=False)
```

time: 267 us -> 69.6 us (0.26)
  the two profiles are of different devices: /device:TPU:35 before, /device:TPU:33 now
where the time goes in v1:
time: 69.6 us; the launch traced here: 69.2 us
  starting transfers between devices  28.1 us (40%)
  Pallas kernels  26.5 us (38%)
  waiting for transfers between devices  11 us (16%)
  local copies, waits for them, and re-layouts  2.84 us (4%)
    pallas_call x5, Pallas kernels, call(): pl.pallas_call(kernel, out_shape=[jax.ShapeDtypeStruct(s, d) for s, d in...  26.5 us
    all_to_all x2, starting transfers between devices, exchange_end(): return lax.all_to_all(message, AXES, 1, 1, axis_index_groups=groups)  21.4 us
    ppermute x2, starting transfers between devices, exchange_start(): return lax.ppermute(other, AXES, pairs)  6.72 us
    ppermute x2, waiting for transfers between devices, exchange_start(): return lax.ppermute(other, AXES, pairs)  6.01 us
    all_to_all x2, waiting for transfers between devices, exchange_end(): return lax.all_to_all(message, AXES, 1, 1, axis_index_groups=groups)  4.98 us
    all_to_all x2, local copies, waits for them, and re-layouts, exchange_end(): return lax.all_to_all(message, AXES, 1, 1, axis_index_groups=groups)  1.42 us
    another operation x2, local copies, waits for them, and re-layouts, exchange_end(): message = jnp.stack([main, jnp.concatenate([relay, relay], axis=0)])  1.41 us
  transfers between devices with their start and end apart: 4, of which 4 were waited for; matrix products, arithmetic and copies ran while one was open for 0% of the time, Pallas kernels for 12%

profile of v1, /device:TPU:33, one launch (start us, length us, event | category | flops | bytes accessed | tf_op | source)
XLA Modules:
  0.0 69.2 jit_solution(643660703307909350)
XLA Ops:
  0.0 0.6 pad_add_fusion.ids
  0.6 6.7 %predict.1 = (f32[243,128]{1,0:T(8,128)}, f32[56,1152]{1,0:T(8,128)}, f32[56,1152]{1,0:T(8,128)}, f32[4,8,512]{2,1,0:T(8,128)}, f32[8,8,512]{2,1,0:T(8,128)}, /*index=5*/bf16[168,192]{1,0:T(8,128)(2,1)}) custom-call(s32[2]{0:T(128)} %pad_add_fusion.ids, f32[9,56,128]{2,1,0:T(8,128)} %bitcast.24, f32[3,56,56]{2,1,0:T(8,128)} %stiff.3, f32[81,3,16]{2,1,0:T(4,128)} %bitcast.31, ...), custom_call_target="tpu_custom_call" | custom-call | tf_op jit(solution)/shard_map/predict/pallas_call | solution.py:311
  7.3 0.0 copy-start.1
  7.3 4.7 %collective-permute-start = (f32[4,8,512]{2,1,0:T(8,128)}, f32[4,8,512]{2,1,0:T(8,128)S(1)}, u32[]{:S(2)}, u32[]{:S(2)}) collective-permute-start(f32[4,8,512]{2,1,0:T(8,128)} %get-tuple-element.26), channel_id=1, source_target_pairs={{4,8},{8,4},{5,9},{9,5},{6,10},{10,6},{7,11},{11,7},{12,16},{16,12... | collective-permute-start | bytes 196616 | tf_op jit(solution)/shard_map/ppermute | solution.py:326
  12.0 2.1 %collective-permute-done = f32[4,8,512]{2,1,0:T(8,128)S(1)} collective-permute-done((f32[4,8,512]{2,1,0:T(8,128)}, f32[4,8,512]{2,1,0:T(8,128)S(1)}, u32[]{:S(2)}, u32[]{:S(2)}) %collective-permute-start) | collective-permute-done | bytes 65568 | tf_op jit(solution)/shard_map/ppermute | solution.py:326
  14.1 0.0 copy-done.1
  14.2 0.7 %copy.16 = f32[2,8,8,512]{3,2,0,1:T(8,128)} copy(f32[2,8,8,512]{3,2,1,0:T(8,128)S(1)} %pad_maximum_fusion) | data formatting | bytes 524288 | tf_op jit(solution)/shard_map/stack | solution.py:331
  14.9 14.4 %all-to-all-start = ((f32[2,8,8,512]{3,2,0,1:T(8,128)}), f32[2,8,8,512]{3,2,0,1:T(8,128)S(1)}, u32[]{:S(2)}, u32[]{:S(2)}) async-start(f32[2,8,8,512]{3,2,0,1:T(8,128)} %copy.16), calls=%async_computation | async-start | bytes 524288 | tf_op jit(solution)/shard_map/all_to_all | solution.py:332
  29.3 4.3 %window_a.1 = (f32[56,1152]{1,0:T(8,128)}, f32[224,512]{1,0:T(8,128)}, bf16[512,512]{1,0:T(8,128)(2,1)}, bf16[512,512]{1,0:T(8,128)(2,1)}, bf16[264,192]{1,0:T(8...) custom-call(f32[56,1152]{1,0:T(8,128)} %get-tuple-element.27.first, f32[9,56,128]{2,1,0:T(8,128)} %bitcast.25, ...), custom_call_target="tpu_custom_call" | custom-call | tf_op jit(solution)/shard_map/window_a/pallas_call | solution.py:311
  33.6 2.2 %all-to-all-done = f32[2,8,8,512]{3,2,0,1:T(8,128)S(1)} async-done(((f32[2,8,8,512]{3,2,0,1:T(8,128)}), f32[2,8,8,512]{3,2,0,1:T(8,128)S(1)}, u32[]{:S(2)}, u32[]{:S(2)}) %all-to-all-start) | async-done | bytes 262176 | tf_op jit(solution)/shard_map/all_to_all | solution.py:332
  35.8 0.7 %copy.17.recv = f32[2,8,8,512]{3,2,1,0:T(8,128)} copy(f32[2,8,8,512]{3,2,0,1:T(8,128)S(1)} %all-to-all-done) | data formatting | bytes 524288 | tf_op jit(solution)/shard_map/all_to_all | solution.py:332
  36.5 8.0 %middle.1 = (f32[56,1152]{1,0:T(8,128)}, f32[56,1152]{1,0:T(8,128)}, f32[56,1152]{1,0:T(8,128)}, f32[4,8,512]{2,1,0:T(8,128)}, f32[8,8,512]{2,1,0:T(8,128)}) custom-call(s32[2]{0:T(128)} %pad_add_fusion.ids, f32[2,8,8,512]{3,2,1,0:T(8,128)} %copy.17.recv, f32[224,512]{1,0:T(8,128)} %get-tuple-element.29.chosen, ...), custom_call_target="tpu_custom_call" | custom-call | tf_op jit(solution)/shard_map/middle/pallas_call | solution.py:311
  44.5 0.0 copy-start
  44.5 2.0 %collective-permute-start.1 = (f32[4,8,512]{2,1,0:T(8,128)}, f32[4,8,512]{2,1,0:T(8,128)S(1)}, u32[]{:S(2)}, u32[]{:S(2)}) collective-permute-start(f32[4,8,512]{2,1,0:T(8,128)} %get-tuple-element.37), channel_id=1, source_target_pairs={{4,8},{8,4},{5,9},{9,5},{6,10},{10,6},{7,11},{11,7},{12,16},{16,12... | collective-permute-start | bytes 196616 | tf_op jit(solution)/shard_map/ppermute | solution.py:326
  46.6 3.9 %collective-permute-done.1 = f32[4,8,512]{2,1,0:T(8,128)S(1)} collective-permute-done((f32[4,8,512]{2,1,0:T(8,128)}, f32[4,8,512]{2,1,0:T(8,128)S(1)}, u32[]{:S(2)}, u32[]{:S(2)}) %collective-permute-start.1) | collective-permute-done | bytes 65568 | tf_op jit(solution)/shard_map/ppermute | solution.py:326
  50.5 0.0 copy-done
  50.5 0.7 %copy.18 = f32[2,8,8,512]{3,2,0,1:T(8,128)} copy(f32[2,8,8,512]{3,2,1,0:T(8,128)S(1)} %pad_maximum_fusion.1) | data formatting | bytes 524288 | tf_op jit(solution)/shard_map/stack | solution.py:331
  51.2 7.0 %all-to-all-start.1 = ((f32[2,8,8,512]{3,2,0,1:T(8,128)}), f32[2,8,8,512]{3,2,0,1:T(8,128)S(1)}, u32[]{:S(2)}, u32[]{:S(2)}) async-start(f32[2,8,8,512]{3,2,0,1:T(8,128)} %copy.18), calls=%async_computation.1 | async-start | bytes 524288 | tf_op jit(solution)/shard_map/all_to_all | solution.py:332
  58.2 3.8 %window_b.1 = (f32[56,1152]{1,0:T(8,128)}, f32[224,512]{1,0:T(8,128)}) custom-call(f32[56,1152]{1,0:T(8,128)} %get-tuple-element.38.later, f32[56,1152]{1,0:T(8,128)} %get-tuple-element.39.own, f32[56,1152]{1,0:T(8,128)} %get-tuple-element.40.part, f32[243,128]{1,0:T(8,128)} %get-tuple-element.28.star, f32[81,4,128]{2,1,0:T(4,128)} %bitcast.28, ...), custom_call_target="tpu_custom_call" | custom-call | tf_op jit(solution)/shard_map/window_b/pallas_call | solution.py:311
  62.0 2.8 %all-to-all-done.1 = f32[2,8,8,512]{3,2,0,1:T(8,128)S(1)} async-done(((f32[2,8,8,512]{3,2,0,1:T(8,128)}), f32[2,8,8,512]{3,2,0,1:T(8,128)S(1)}, u32[]{:S(2)}, u32[]{:S(2)}) %all-to-all-start.1) | async-done | bytes 262176 | tf_op jit(solution)/shard_map/all_to_all | solution.py:332
  64.8 0.7 %copy.19.recv = f32[2,8,8,512]{3,2,1,0:T(8,128)} copy(f32[2,8,8,512]{3,2,0,1:T(8,128)S(1)} %all-to-all-done.1) | data formatting | bytes 524288 | tf_op jit(solution)/shard_map/all_to_all | solution.py:332
  65.5 3.7 %final.1 = f32[9,56,128]{2,1,0:T(8,128)} custom-call(s32[2]{0:T(128)} %pad_add_fusion.ids, f32[2,8,8,512]{3,2,1,0:T(8,128)} %copy.19.recv, f32[224,512]{1,0:T(8,128)} %get-tuple-element.43.chosen, bf16[512,512]{1,0:T(8,128)(2,1)} %get-tuple-element.30.hot_ghost, bf16[264,192]{1,0:T(8,128)(2,1)} %get-tuple-element.31.both, ...), custom_call_target="tpu_custom_call" | custom-call | tf_op jit(solution)/shard_map/final/pallas_call | solution.py:311
  (4 shorter events, 0.1 us)
Async XLA Ops:
  7.3 6.8 %copy-start.1 = (f32[8,8,512]{2,1,0:T(8,128)S(1)}, f32[8,8,512]{2,1,0:T(8,128)}, u32[]{:S(2)}) copy-start(f32[8,8,512]{2,1,0:T(8,128)} %get-tuple-element.25) | copy-start | bytes 393220
  7.3 6.8 %collective-permute-start = (f32[4,8,512]{2,1,0:T(8,128)}, f32[4,8,512]{2,1,0:T(8,128)S(1)}, u32[]{:S(2)}, u32[]{:S(2)}) collective-permute-start(f32[4,8,512]{2,1,0:T(8,128)} %get-tuple-element.26), channel_id=1, source_target_pairs={{4,8},{8,4},{5,9},{9,5},{6,10},{10,6},{7,11},{11,7},{12,16},{16,12... | collective-permute-start | bytes 196616 | tf_op jit(solution)/shard_map/ppermute | solution.py:326
  14.9 20.9 %all-to-all-start = ((f32[2,8,8,512]{3,2,0,1:T(8,128)}), f32[2,8,8,512]{3,2,0,1:T(8,128)S(1)}, u32[]{:S(2)}, u32[]{:S(2)}) async-start(f32[2,8,8,512]{3,2,0,1:T(8,128)} %copy.16), calls=%async_computation | async-start | bytes 524288 | tf_op jit(solution)/shard_map/all_to_all | solution.py:332
  44.5 5.9 %copy-start = (f32[8,8,512]{2,1,0:T(8,128)S(1)}, f32[8,8,512]{2,1,0:T(8,128)}, u32[]{:S(2)}) copy-start(f32[8,8,512]{2,1,0:T(8,128)} %get-tuple-element.36) | copy-start | bytes 393220
  44.5 5.9 %collective-permute-start.1 = (f32[4,8,512]{2,1,0:T(8,128)}, f32[4,8,512]{2,1,0:T(8,128)S(1)}, u32[]{:S(2)}, u32[]{:S(2)}) collective-permute-start(f32[4,8,512]{2,1,0:T(8,128)} %get-tuple-element.37), channel_id=1, source_target_pairs={{4,8},{8,4},{5,9},{9,5},{6,10},{10,6},{7,11},{11,7},{12,16},{16,12... | collective-permute-start | bytes 196616 | tf_op jit(solution)/shard_map/ppermute | solution.py:326
  51.2 13.5 %all-to-all-start.1 = ((f32[2,8,8,512]{3,2,0,1:T(8,128)}), f32[2,8,8,512]{3,2,0,1:T(8,128)S(1)}, u32[]{:S(2)}, u32[]{:S(2)}) async-start(f32[2,8,8,512]{3,2,0,1:T(8,128)} %copy.18), calls=%async_computation.1 | async-start | bytes 524288 | tf_op jit(solution)/shard_map/all_to_all | solution.py:332

commit v2 on v1

--- a/solution.py
+++ b/solution.py
@@ -78,8 +78,11 @@
                 moved[order % 2, :, cols] = dot32(lhs[...], rhs[:, cols])
 
 
-def pack_blocks(ids, send, payload, gat, res, trans, other, main):
-    slots = jnp.concatenate([send[...], jnp.full((1, EL - send.shape[1]), -1, jnp.int32)], axis=1)
+def send_slots(send):
+    return jnp.concatenate([send[...], jnp.full((1, EL - send.shape[1]), -1, jnp.int32)], axis=1)
+
+
+def pack_blocks(slots, payload, gat, res, trans, other, main):
     rows = lax.broadcasted_iota(jnp.int32, (EL, EL), 0)
     pick = jnp.where(rows == slots, 1.0, 0.0).astype(BF16)
     pick = jnp.concatenate([pick, pick], axis=0)
@@ -93,7 +96,7 @@
         res[q * NB : (q + 1) * NB, :] = got[q * 64 : q * 64 + NB]
     res[NF * NB : 512, :] = jnp.zeros((8, EL), F32)
     trans[...] = res[...].T
-    core = ids[0]
+    core = lax.axis_index("dom") % 2
     for r in range(4):
         other[r] = trans[pl.ds(pl.multiple_of(8 * (2 * core * 4 + r), 8), 8), :]
     for c in range(2):
@@ -101,7 +104,10 @@
             main[c * 4 + r] = trans[pl.ds(pl.multiple_of(8 * ((c - core + 1) * 4 + r), 8), 8), :]
 
 
-def k_predict(ids, dof, stiff, jac, mat, inv, send, star, first, second, other, main, lhs_out, lhs, rhs, moved, gat, res, trans):
+def k_predict(mat, jac, inv, stiff, dof, send, star, first, second, other, main, lhs_out, lhs, rhs, moved, gat, res, trans):
+    mat, jac, inv = mat.ready(), jac.ready(), inv.ready()
+    star_out, first_out, second_out = star, first, second
+    star, first, second = star.ref, first.ref, second.ref
     pick = (lax.broadcasted_iota(jnp.int32, (16, EL), 0) == mat[...]).astype(F32)
     per = [jnp.dot(jac[:, c, :], pick, precision=HIGH, preferred_element_type=F32) for c in range(3)]
     for d in range(3):
@@ -110,10 +116,14 @@
             t = per[c] * inv[c, pl.ds(d, 1), :]
             total = t if total is None else total + t
         star[d * 81 : (d + 1) * 81, :] = total
+    star_out.flush()
+    stiff = stiff.ready()
     lhs[...] = jnp.zeros(lhs.shape, BF16)
     for d in range(3):
         put_lhs(lhs, slice(d * NB, (d + 1) * NB), -(stiff[d].T))
-    lhs_out[...] = lhs[...]
+    lhs_out.ref[...] = lhs[...]
+    lhs_out.flush()
+    dof = dof.ready()
     for p in range(NF):
         x = dof[p]
         put_rhs(rhs, field(p), x)
@@ -126,7 +136,9 @@
         second[:, field(p)] = second[:, field(p)] + ((2 ** (order + 1) - 1) * scale) * block
 
     run_series(lhs, rhs, moved, star, add)
-    pack_blocks(ids, send, first, gat, res, trans, other, main)
+    first_out.flush()
+    second_out.flush()
+    pack_blocks(send_slots(send.ready()), first, gat, res, trans, other.ref, main.ref)
 
 
 def face_mix(source, flux, face, p, lane):
@@ -154,21 +166,50 @@
             put(p, block + lifted[:, n * EL : (n + 1) * EL])
 
 
-def gather_table(source, table):
+def gather_table(source, table, table_f):
     for q in range(NF):
         for j in range(4):
-            table[q * FP : (q + 1) * FP, j * EL : (j + 1) * EL] = source(j, q)
-    table[NF * FP : 224, :] = jnp.zeros((8, 4 * EL), F32)
+            table_f[q * FP : (q + 1) * FP, j * EL : (j + 1) * EL] = source(j, q)
+    table_f[NF * FP : 224, :] = jnp.zeros((8, 4 * EL), F32)
+    hi, lo = halves(table_f[...])
+    table[0:224, :] = hi
+    table[224:448, :] = lo
 
 
 def gather_from(table, hot):
-    hi, lo = halves(table[...])
-    return dot32(hi, hot) + dot32(lo, hot)
-
-
-def k_window_a(first, dof, star, stiff, proj, lift, rotate, flux_own, nbr, across,
-               base, chosen, hot_own, hot_ghost, both, lift_own, lift_rot,
-               rhs, moved, solved, table, lift_f, rot_f):
+    got = dot32(table[...], hot)
+    return got[0:224] + got[224:448]
+
+
+class Window:
+    def __init__(self, ref, start, stop, width):
+        self.ref, self.start, self.stop, self.width = ref, start, stop, width
+        self.shape = (stop - start, width)
+
+    def place(self, key):
+        key = key if isinstance(key, tuple) else (key,)
+        rows = slice(None) if key[0] is Ellipsis else key[0]
+        cols = key[1] if len(key) > 1 else slice(None)
+        first, last, _ = rows.indices(self.stop - self.start)
+        left, right, _ = cols.indices(self.width)
+        return slice(self.start + first, self.start + last), slice(left, right)
+
+    def __getitem__(self, key):
+        return self.ref[self.place(key)]
+
+    def __setitem__(self, key, value):
+        self.ref[self.place(key)] = value
+
+
+def weight_parts(weights):
+    return Window(weights, 0, 264, 192), Window(weights, 264, 432, 192), Window(weights, 432, 544, 288)
+
+
+def k_own_a(stiff, proj, lift, rotate, first, flux_own, star, dof, lhs, second,
+            state, projected, weights, lift_own, rhs, moved, solved, lift_f, rot_f):
+    stiff, proj, lift, rotate = stiff.ready(), proj.ready(), lift.ready(), rotate.ready()
+    state, projected, lift_own = state.ref, projected.ref, lift_own.ref
+    both, lhs_out, lift_rot = weight_parts(weights.ref)
     both[...] = jnp.zeros(both.shape, BF16)
     for d in range(3):
         put_lhs(both, slice(d * NB, (d + 1) * NB), stiff[d])
@@ -189,6 +230,31 @@
     lr_hi, lr_lo = halves(rot_f[...].T)
     lift_rot[0:NB] = lr_hi
     lift_rot[NB : 2 * NB] = lr_lo
+    first = first.ready()
+    for p in range(NF):
+        put_rhs(rhs, field(p), first[:, field(p)])
+    flux_own, star, dof = flux_own.ready(), star.ready(), dof.ready()
+    lhs_out[...] = lhs.ready()[...]
+    weights.flush()
+    state[NB : 2 * NB, :] = first[...]
+    state[2 * NB : 3 * NB, :] = second.ready()[...]
+    for p in range(NF):
+        state[3 * NB : 4 * NB, field(p)] = dof[p]
+
+    def put(p, block):
+        state[0:NB, field(p)] = dof[p] + block
+
+    own_terms(both, rhs, moved, star, flux_own, lift_own, solved, put)
+    projected[...] = moved[3 * NB :, :]
+
+
+def k_pick_a(nbr, across, projected, rot, cluster, send, chosen, hot_own, hot_ghost, marks, table, table_f):
+    marks.ref[0:4, :] = rot.ready()[...]
+    marks.ref[4:5, :] = cluster.ready()[...]
+    marks.ref[5:6, :] = send_slots(send.ready())
+    nbr, across = nbr.ready(), across.ready()
+    chosen, hot_own_out, hot_ghost_out = chosen.ref, hot_own, hot_ghost
+    hot_own, hot_ghost = hot_own.ref, hot_ghost.ref
     rows = lax.broadcasted_iota(jnp.int32, (EL, EL), 0)
     for i in range(4):
         n = nbr[pl.ds(i, 1), :]
@@ -196,54 +262,63 @@
         for j in range(4):
             hot_own[j * EL : (j + 1) * EL, field(i)] = jnp.where(rows + j * EL == key, 1.0, 0.0).astype(BF16)
             hot_ghost[j * EL : (j + 1) * EL, field(i)] = jnp.where(rows + (j + 4) * EL == key, 1.0, 0.0).astype(BF16)
-    for p in range(NF):
-        put_rhs(rhs, field(p), first[:, field(p)])
+    hot_own_out.flush()
+    hot_ghost_out.flush()
+    projected = projected.ready()
+    gather_table(lambda j, q: projected[j * FP : (j + 1) * FP, field(q)], table, table_f)
+    chosen[...] = gather_from(table, hot_own[...])
+
+
+def k_own_b(own, weights, flux_own, lift_own, star, part, later, base, rhs, moved, solved):
+    own, base = own.ready(), base.ref
+    for p in range(NF):
+        put_rhs(rhs, field(p), own[:, field(p)])
+    both = weight_parts(weights.ready())[0]
+    flux_own, lift_own, star, part = flux_own.ready(), lift_own.ready(), star.ready(), part.ready()
 
     def put(p, block):
-        base[:, field(p)] = dof[p] + block
+        base[:, field(p)] = part[:, field(p)] + block
 
     own_terms(both, rhs, moved, star, flux_own, lift_own, solved, put)
-    gather_table(lambda j, q: moved[3 * NB + j * FP : 3 * NB + (j + 1) * FP, field(q)], table)
-    chosen[...] = gather_from(table, hot_own[...])
-
-
-def k_window_b(later, own, part, star, flux_own, hot_own, both, lift_own,
-               base, chosen, rhs, moved, solved, table, proj_b):
+
+
+def k_pick_b(later, weights, hot_own, base, chosen, rhs, proj_b, table, table_f):
+    later, chosen = later.ready(), chosen.ref
     for p in range(NF):
         put_rhs(rhs, field(p), later[:, field(p)])
+    both = weight_parts(weights.ready())[0]
     for group in PAIRS:
         cols = pair_cols(group)
         proj_b[:, cols] = dot32(both[3 * NB :, :], rhs[:, cols])
-    gather_table(lambda j, q: proj_b[j * FP : (j + 1) * FP, field(q)], table)
+    gather_table(lambda j, q: proj_b[j * FP : (j + 1) * FP, field(q)], table, table_f)
+    hot_own = hot_own.ready()
     chosen[...] = gather_from(table, hot_own[...])
-    for p in range(NF):
-        put_rhs(rhs, field(p), own[:, field(p)])
-
-    def put(p, block):
-        base[:, field(p)] = part[:, field(p)] + block
-
-    own_terms(both, rhs, moved, star, flux_own, lift_own, solved, put)
-
-
-def near_terms(ids, recv, chosen, hot_ghost, both, lift_rot, flux_across, rot,
-               ghost, ghost_t, rhs, proj_g, table, near, solved, turned, put):
-    core = ids[0]
-    pos = ids[1]
+
+
+def near_terms(recv, chosen, hot_ghost, weights, flux_across, marks,
+               ghost, ghost_t, rhs, proj_g, table, table_f, near, solved, turned, settle, put):
+    core = lax.axis_index("dom") % 2
+    pos = lax.axis_index("sub")
+    recv = recv.ready()
     for s in range(4):
         keep = jnp.where(pos == s, 0.0, 1.0).astype(F32)
-        ghost[(4 + s) * 8 : (5 + s) * 8, :] = recv[0, core * 4 + s] * keep
+        ghost[(4 + s) * 8 : (5 + s) * 8, :] = recv[core * 4 + s, 0] * keep
         row = pl.multiple_of(8 * ((2 - 2 * core) * 4 + s), 8)
-        ghost[pl.ds(row, 8), :] = recv[0, (1 - core) * 4 + s]
+        ghost[pl.ds(row, 8), :] = recv[(1 - core) * 4 + s, 0]
         row = pl.multiple_of(8 * (2 * core * 4 + s), 8)
-        ghost[pl.ds(row, 8), :] = recv[1, core * 4 + s]
+        ghost[pl.ds(row, 8), :] = recv[core * 4 + s, 1]
     ghost[96:EL, :] = jnp.zeros((EL - 96, 512), F32)
     ghost_t[...] = ghost[...].T
     for q in range(NF):
         put_rhs(rhs, field(q), ghost_t[q * NB : (q + 1) * NB, :])
+    both, _, lift_rot = weight_parts(weights.ready())
     for group in PAIRS:
         cols = pair_cols(group)
         proj_g[:, cols] = dot32(both[3 * NB :, :], rhs[:, cols])
-    gather_table(lambda j, q: proj_g[j * FP : (j + 1) * FP, field(q)], table)
+    gather_table(lambda j, q: proj_g[j * FP : (j + 1) * FP, field(q)], table, table_f)
+    hot_ghost, chosen = hot_ghost.ready(), chosen.ready()
+    flux_across, rot = flux_across.ready(), marks.ready()
+    settle()
     near[...] = chosen[...] + gather_from(table, hot_ghost[...])
     for p in range(NF):
         for i in range(4):
@@ -264,21 +339,31 @@
         put(group, top[0:NB] + top[NB : 2 * NB] + dot32(lift_rot[0:NB, :], turned[1, :, cols]))
 
 
-def k_middle(ids, recv, chosen, hot_ghost, both, lift_rot, flux_across, rot, base, lhs, star, first, second, dof, cluster, send,
+def k_middle(recv, weights, hot_ghost, chosen, flux_across, marks, state, star,
              later, own, part, other, main,
-             ghost, ghost_t, rhs, proj_g, table, near, solved, turned, moved, total, gat, res):
-    fine = cluster[...] == 0
+             ghost, ghost_t, rhs, proj_g, table, table_f, near, solved, turned, moved, total, gat, res):
+    box = {}
+    later_out, own_out, part_out = later, own, part
+    later, own, part = later.ref, own.ref, part.ref
+
+    def settle():
+        box["state"] = state.ready()
+        box["fine"] = marks.ready()[4:5, :] == 0
 
     def put(group, block):
         for n, p in enumerate(group):
             b = block[:, n * EL : (n + 1) * EL]
-            stepped = base[:, field(p)] + b
-            part[:, field(p)] = jnp.where(fine, stepped, dof[p] + b)
+            stepped = box["state"][0:NB, field(p)] + b
+            part[:, field(p)] = jnp.where(box["fine"], stepped, box["state"][3 * NB : 4 * NB, field(p)] + b)
             total[:, field(p)] = stepped
             put_rhs(rhs, field(p), stepped)
 
-    near_terms(ids, recv, chosen, hot_ghost, both, lift_rot, flux_across, rot,
-               ghost, ghost_t, rhs, proj_g, table, near, solved, turned, put)
+    near_terms(recv, chosen, hot_ghost, weights, flux_across, marks,
+               ghost, ghost_t, rhs, proj_g, table, table_f, near, solved, turned, settle, put)
+    part_out.flush()
+    fine = box["fine"]
+    star, state = star.ready(), state.ready()
+    lhs = weight_parts(weights.ready())[1]
 
     def add(order, p, block):
         scale = 1.0 / math.factorial(order + 1)
@@ -286,34 +371,109 @@
         if order < ORDER - 1:
             total[:, field(p)] = t
         else:
-            sec = second[:, field(p)]
+            sec = state[2 * NB : 3 * NB, field(p)]
             later[:, field(p)] = jnp.where(fine, t, sec)
-            own[:, field(p)] = jnp.where(fine, t, first[:, field(p)] + sec)
+            own[:, field(p)] = jnp.where(fine, t, state[NB : 2 * NB, field(p)] + sec)
 
     run_series(lhs, rhs, moved, star, add)
-    pack_blocks(ids, send, later, gat, res, ghost, other, main)
-
-
-def k_final(ids, recv, chosen, hot_ghost, both, lift_rot, flux_across, rot, base, out,
-            ghost, ghost_t, rhs, proj_g, table, near, solved, turned):
+    later_out.flush()
+    own_out.flush()
+    pack_blocks(marks.ready()[5:6, :], later, gat, res, ghost, other.ref, main.ref)
+
+
+def k_final(recv, weights, hot_ghost, chosen, flux_across, marks, base, out,
+            ghost, ghost_t, rhs, proj_g, table, table_f, near, solved, turned):
+    box = {}
+
+    def settle():
+        box["base"] = base.ready()
+
     def put(group, block):
         for n, p in enumerate(group):
-            out[p] = base[:, field(p)] + block[:, n * EL : (n + 1) * EL]
-
-    near_terms(ids, recv, chosen, hot_ghost, both, lift_rot, flux_across, rot,
-               ghost, ghost_t, rhs, proj_g, table, near, solved, turned, put)
-
-
-def call(kernel, name, outs, scratch, smem_first, *args):
-    space = [pl.BlockSpec(memory_space=pltpu.VMEM) for _ in args]
-    if smem_first:
-        space[0] = pl.BlockSpec(memory_space=pltpu.SMEM)
+            out.ref[p] = box["base"][:, field(p)] + block[:, n * EL : (n + 1) * EL]
+
+    near_terms(recv, chosen, hot_ghost, weights, flux_across, marks,
+               ghost, ghost_t, rhs, proj_g, table, table_f, near, solved, turned, settle, put)
+
+
+class Held:
+    def __init__(self, source, ref, sem):
+        self.ref = ref
+        self.copy = pltpu.make_async_copy(source, ref, sem)
+        self.waited = False
+        self.copy.start()
+
+    def ready(self):
+        if not self.waited:
+            self.copy.wait()
+            self.waited = True
+        return self.ref
+
+
+class Result:
+    def __init__(self, target, ref, sem):
+        self.ref = ref
+        self.copy = pltpu.make_async_copy(ref, target, sem)
+        self.flushed = False
+
+    def flush(self):
+        if not self.flushed:
+            self.copy.start()
+            self.flushed = True
+
+
+class Direct:
+    def __init__(self, ref):
+        self.ref = ref
+
+    def ready(self):
+        return self.ref
+
+    def flush(self):
+        pass
+
+
+def call_direct(kernel, name, outs, scratch, *args):
+    n, m = len(args), len(outs)
+
+    def body(*refs):
+        kernel(*[Direct(r) for r in refs[: n + m]], *refs[n + m :])
+
     return pl.pallas_call(
-        kernel,
+        body,
         out_shape=[jax.ShapeDtypeStruct(s, d) for s, d in outs],
-        in_specs=space,
+        in_specs=[pl.BlockSpec(memory_space=pltpu.VMEM) for _ in args],
         out_specs=[pl.BlockSpec(memory_space=pltpu.VMEM) for _ in outs],
         scratch_shapes=[pltpu.VMEM(s, d) for s, d in scratch],
+        compiler_params=pltpu.CompilerParams(vmem_limit_bytes=24 * 2**20),
+        name=name,
+    )(*args)
+
+
+def call(kernel, name, outs, scratch, *args):
+    n, m = len(args), len(outs)
+
+    def body(*refs):
+        sems_in, sems_out = refs[-2:]
+        held = refs[n + m : 2 * (n + m)]
+        ins = [Held(refs[k], held[k], sems_in.at[k]) for k in range(n)]
+        results = [Result(refs[n + k], held[n + k], sems_out.at[k]) for k in range(m)]
+        kernel(*ins, *results, *refs[2 * (n + m) : -2])
+        for r in results:
+            r.flush()
+        for a in ins:
+            a.ready()
+        for r in results:
+            r.copy.wait()
+
+    buffers = [pltpu.VMEM(a.shape, a.dtype) for a in args] + [pltpu.VMEM(s, d) for s, d in outs]
+    return pl.pallas_call(
+        body,
+        out_shape=[jax.ShapeDtypeStruct(s, d) for s, d in outs],
+        in_specs=[pl.BlockSpec(memory_space=pl.ANY) for _ in args],
+        out_specs=[pl.BlockSpec(memory_space=pl.ANY) for _ in outs],
+        scratch_shapes=[*buffers, *[pltpu.VMEM(s, d) for s, d in scratch],
+                        pltpu.SemaphoreType.DMA((n,)), pltpu.SemaphoreType.DMA((m,))],
         name=name,
     )(*args)
 
@@ -328,14 +488,13 @@
 
 def exchange_end(relay, main, slabs):
     groups = [[(2 * c + b) * 4 + s for b in range(2) for s in range(4)] for c in range(slabs // 2)]
-    message = jnp.stack([main, jnp.concatenate([relay, relay], axis=0)])
-    return lax.all_to_all(message, AXES, 1, 1, axis_index_groups=groups)
+    message = jnp.stack([main, jnp.concatenate([relay, relay], axis=0)], axis=1)
+    return lax.all_to_all(message, AXES, 0, 0, axis_index_groups=groups)
 
 
 def local(dof_state, stiffness, face_proj, face_lift, face_rotate, jacobians, material, inv_jacobian,
           flux_own, flux_across, cluster, neighbour, across_face, rotation, send_list):
     slabs = lax.axis_size("dom")
-    ids = jnp.stack([lax.axis_index("dom") % 2, lax.axis_index("sub")]).astype(jnp.int32)
     dof = jnp.transpose(dof_state, (1, 0, 2))
     jac = jnp.transpose(jacobians, (2, 3, 1, 0)).reshape(81, 3, 16)
     proj = jnp.transpose(face_proj, (1, 0, 2))
@@ -350,32 +509,38 @@
     rhs = ((192, WID), BF16)
     pack = [((576, 2 * EL), BF16), ((512, EL), F32), ((EL, 512), F32)]
     star, first, second, other, main, lhs = call(
-        k_predict, "predict", [((243, EL), F32), state, state, *blocks, ((168, 192), BF16)],
+        k_predict, "predict",
+        [((243, EL), F32), state, state, *blocks, ((168, 192), BF16)],
         [((168, 192), BF16), rhs, ((2, 168, WID), F32), *pack],
-        True, ids, dof, stiffness, jac, mat, inv_jacobian, send)
+        mat, jac, inv_jacobian, stiffness, dof, send)
     relay = exchange_start(other, slabs)
-    table = ((224, 512), F32)
+    rows = ((224, 512), F32)
     hot = ((512, 512), BF16)
-    base, chosen, hot_own, hot_ghost, both, lift_own, lift_rot = call(
-        k_window_a, "window_a",
-        [state, table, hot, hot, ((264, 192), BF16), ((2, NB, 96), BF16), ((2 * NB, 288), BF16)],
-        [rhs, ((264, WID), F32), ((96, WID), F32), table, ((96, NB), F32), ((288, NB), F32)],
-        False, first, dof, star, stiffness, proj, lift, face_rotate, f_own, neighbour, across_face)
+    tables = [((448, 512), BF16), rows]
+    own_scratch = [rhs, ((264, WID), F32), ((96, WID), F32)]
+    state_pack, projected, weights, lift_own = call(
+        k_own_a, "own_a",
+        [((4 * NB, WID), F32), ((96, WID), F32), ((544, 288), BF16), ((2, NB, 96), BF16)],
+        [*own_scratch, ((96, NB), F32), ((288, NB), F32)],
+        stiffness, proj, lift, face_rotate, first, f_own, star, dof, lhs, second)
+    relay, projected = lax.optimization_barrier((relay, projected))
+    chosen, hot_own, hot_ghost, marks = call_direct(
+        k_pick_a, "pick_a", [rows, hot, hot, ((8, EL), jnp.int32)], tables,
+        neighbour, across_face, projected, rotation, clu, send)
     recv = exchange_end(relay, main, slabs)
-    near_scratch = [((EL, 512), F32), ((512, EL), F32), rhs, ((96, WID), F32), table, table, ((96, WID), F32), ((2, 288, WID), BF16)]
-    later, own, part, other, main = call(
+    near_scratch = [((EL, 512), F32), ((512, EL), F32), rhs, ((96, WID), F32), *tables, rows, ((96, WID), F32), ((2, 288, WID), BF16)]
+    later, own, part, other, main = call_direct(
         k_middle, "middle", [state, state, state, *blocks],
         [*near_scratch, ((2, 168, WID), F32), state, pack[0], pack[1]],
-        True, ids, recv, chosen, hot_ghost, both, lift_rot, f_across, rotation, base, lhs, star, first, second, dof, clu, send)
+        recv, weights, hot_ghost, chosen, f_across, marks, state_pack, star)
     relay = exchange_start(other, slabs)
-    base, chosen = call(
-        k_window_b, "window_b", [state, table],
-        [rhs, ((264, WID), F32), ((96, WID), F32), table, ((96, WID), F32)],
-        False, later, own, part, star, f_own, hot_own, both, lift_own)
+    (base,) = call_direct(k_own_b, "own_b", [state], own_scratch, own, weights, f_own, lift_own, star, part, later)
+    relay, base, later = lax.optimization_barrier((relay, base, later))
+    (chosen,) = call_direct(k_pick_b, "pick_b", [rows], [rhs, ((96, WID), F32), *tables], later, weights, hot_own, base)
     recv = exchange_end(relay, main, slabs)
-    (out,) = call(
+    (out,) = call_direct(
         k_final, "final", [((NF, NB, EL), F32)], near_scratch,
-        True, ids, recv, chosen, hot_ghost, both, lift_rot, f_across, rotation, base)
+        recv, weights, hot_ghost, chosen, f_across, marks, base)
     return jnp.transpose(out, (1, 0, 2))
 
 

time: 69.6 us -> 65.7 us (0.944)
  Pallas kernels: 26.5 us -> 21.2 us
  waiting for transfers between devices: 11 us -> 12.5 us
  local copies, waits for them, and re-layouts: 2.84 us -> 1.86 us
  other arithmetic: 0.68 us -> 1.46 us
    pallas_call x5 -> x7, Pallas kernels: 26.5 us -> 21.2 us  [the longest x2 10.9 us: call(): pl.pallas_call(body, out_shape=[jax.ShapeDtypeStruct(s, d) for s, d in ou...]
    all_to_all x2, waiting for transfers between devices: 4.98 us -> 10 us  [exchange_end(): return lax.all_to_all(message, AXES, 0, 0, axis_index_groups=groups)]
    ppermute x2, waiting for transfers between devices: 6.01 us -> 2.46 us  [exchange_start(): return lax.ppermute(other, AXES, pairs)]
    unnamed x4 -> x30, local copies, waits for them, and re-layouts: 0.01 us -> 1.86 us
    all_to_all x2 -> x0, local copies, waits for them, and re-layouts: 1.42 us -> none  [exchange_end(): return lax.all_to_all(message, AXES, 1, 1, axis_index_groups=groups)]
    another operation x2 -> x0, local copies, waits for them, and re-layouts: 1.41 us -> none  [exchange_end(): message = jnp.stack([main, jnp.concatenate([relay, relay], axis=0)])]
    another operation x5 -> x4, other arithmetic: 0.68 us -> 1.46 us  [exchange_end(): message = jnp.stack([main, jnp.concatenate([relay, relay], axis=0)], axis=1)]
  transfers between devices with their start and end apart: 4 -> 4, of which waited for: 4 -> 3; matrix products, arithmetic and copies ran while one was open for 0% -> 0% of each run, Pallas kernels for 12% -> 10%
where the time goes in v2:
time: 65.7 us; the launch traced here: 65.2 us
  starting transfers between devices  27.9 us (42%)
  Pallas kernels  21.2 us (32%)
  waiting for transfers between devices  12.5 us (19%)
  local copies, waits for them, and re-layouts  1.86 us (3%)
  other arithmetic  1.46 us (2%)
    all_to_all x2, starting transfers between devices, exchange_end(): return lax.all_to_all(message, AXES, 0, 0, axis_index_groups=groups)  21.5 us
    pallas_call x2, Pallas kernels, call(): pl.pallas_call(body, out_shape=[jax.ShapeDtypeStruct(s, d) for s, d in ou...  10.9 us
    pallas_call x5, Pallas kernels, call_direct(): pl.pallas_call(body, out_shape=[jax.ShapeDtypeStruct(s, d) for s, d in ou...  10.3 us
    all_to_all x2, waiting for transfers between devices, exchange_end(): return lax.all_to_all(message, AXES, 0, 0, axis_index_groups=groups)  10 us
    ppermute x2, starting transfers between devices, exchange_start(): return lax.ppermute(other, AXES, pairs)  6.48 us
    ppermute x2, waiting for transfers between devices, exchange_start(): return lax.ppermute(other, AXES, pairs)  2.46 us
    unnamed x30, local copies, waits for them, and re-layouts  1.86 us
    another operation x4, other arithmetic, exchange_end(): message = jnp.stack([main, jnp.concatenate([relay, relay], axis=0)], axis=1)  1.46 us
  transfers between devices with their start and end apart: 4, of which 3 were waited for; matrix products, arithmetic and copies ran while one was open for 0% of the time, Pallas kernels for 10%

profile of v2, /device:TPU:33, one launch (start us, length us, event | category | flops | bytes accessed | tf_op | source)
XLA Modules:
  0.0 65.2 jit_solution(16326080316418860604)
XLA Ops:
  0.0 6.8 %predict.1 = (f32[243,128]{1,0:T(8,128)}, f32[56,1152]{1,0:T(8,128)}, f32[56,1152]{1,0:T(8,128)}, f32[4,8,512]{2,1,0:T(8,128)}, f32[8,8,512]{2,1,0:T(8,128)}, /*index=5*/bf16[168,192]{1,0:T(8,128)(2,1)}) custom-call(s32[1,128]{1,0:T(1,128)} %bitcast.36, f32[81,3,16]{2,1,0:T(4,128)} %bitcast.32, f32[3,3,128]{2,1,0:T(4,128)} %refs_2_.1, f32[3,56,56]{2,1,0:T(8,128)} %refs_0_.2, ...), custom_call_target="tpu_custom_call" | custom-call | tf_op jit(solution)/shard_map/predict/pallas_call | solution.py:470
  6.8 4.6 %collective-permute-start = (f32[4,8,512]{2,1,0:T(8,128)}, f32[4,8,512]{2,1,0:T(8,128)S(1)}, u32[]{:S(2)}, u32[]{:S(2)}) collective-permute-start(f32[4,8,512]{2,1,0:T(8,128)} %get-tuple-element.30), channel_id=1, source_target_pairs={{4,8},{8,4},{5,9},{9,5},{6,10},{10,6},{7,11},{11,7},{12,16},{16,12... | collective-permute-start | bytes 196616 | tf_op jit(solution)/shard_map/ppermute | solution.py:486
  11.4 0.0 copy-start.14
  11.4 0.0 copy-start.9
  11.4 0.0 copy-start.10
  11.4 0.0 copy-start.11
  11.5 0.0 copy-start.12
  11.5 0.0 copy-start.13
  11.5 0.0 copy-start.3
  11.5 4.1 %own_a.1 = (f32[224,1152]{1,0:T(8,128)}, f32[96,1152]{1,0:T(8,128)}, bf16[544,288]{1,0:T(8,128)(2,1)}, bf16[2,56,96]{2,1,0:T(8,128)(2,1)}) custom-call(f32[3,56,56]{2,1,0:T(8,128)} %refs_0_.2, f32[21,4,56]{2,1,0:T(4,128)} %bitcast.34, f32[21,4,56]{2,1,0:T(4,128)} %bitcast.35, f32[3,21,21]{2,1,0:T(8,128)} %refs_3_.4, f32[56,1152]{1,0:T(8,128)} %get-tuple-element.31.refs_4_, ...), custom_call_target="tpu_custom_call" | custom-call | tf_op jit(solution)/shard_map/own_a/pallas_call | solution.py:470
  15.6 0.0 copy-start.2
  15.6 0.0 collective-permute-done
  15.6 0.0 copy-done.14
  15.6 0.7 %pad_maximum_fusion = f32[8,2,8,512]{3,2,1,0:T(8,128)} fusion(f32[8,1,8,512]{3,2,1,0:T(8,128)S(1)} %maximum_bitcast_fusion, f32[8,1,8,512]{3,2,1,0:T(8,128)S(1)} %bitcast.33), kind=kLoop, calls=%fused_computation | loop fusion | flops 65536 | bytes 524288 | tf_op jit(solution)/shard_map/stack | solution.py:491
  16.3 0.0 copy-start
  16.3 14.5 %all-to-all-start = ((f32[8,2,8,512]{3,2,1,0:T(8,128)}), f32[8,2,8,512]{3,2,1,0:T(8,128)S(1)}, u32[]{:S(2)}, u32[]{:S(2)}) async-start(f32[8,2,8,512]{3,2,1,0:T(8,128)} %pad_maximum_fusion), calls=%async_computation | async-start | bytes 524288 | tf_op jit(solution)/shard_map/all_to_all | solution.py:492
  30.8 0.0 copy-done.9
  30.8 0.0 copy-done.10
  30.8 0.0 copy-done.11
  30.8 0.0 copy-done.12
  30.8 0.0 copy-done.13
  30.8 0.0 copy-start.7
  30.8 1.0 %copy-done.7 = f32[96,1152]{1,0:T(8,128)S(1)} copy-done((f32[96,1152]{1,0:T(8,128)S(1)}, f32[96,1152]{1,0:T(8,128)}, u32[]{:S(2)}) %copy-start.7) | copy-done | bytes 442392
  31.8 0.0 copy-start.1
  31.8 0.6 pick_a.1
  32.4 0.0 copy-start.5
  32.4 0.8 %copy-done.5 = bf16[512,512]{1,0:T(8,128)(2,1)} copy-done((bf16[512,512]{1,0:T(8,128)(2,1)}, bf16[512,512]{1,0:T(8,128)(2,1)S(1)}, u32[]{:S(2)}) %copy-start.5) | copy-done | bytes 524312
  33.2 4.1 %all-to-all-done.refs_0_ = f32[8,2,8,512]{3,2,1,0:T(8,128)S(1)} async-done(((f32[8,2,8,512]{3,2,1,0:T(8,128)}), f32[8,2,8,512]{3,2,1,0:T(8,128)S(1)}, u32[]{:S(2)}, u32[]{:S(2)}) %all-to-all-start) | async-done | bytes 262176 | tf_op jit(solution)/shard_map/all_to_all | solution.py:492
  37.3 0.0 copy-done.3
  37.3 0.0 copy-done.2
  37.3 0.0 copy-done
  37.3 0.0 copy-done.1
  37.3 0.0 copy-start.4
  37.3 0.0 copy-start.8
  37.4 5.8 %middle.1 = (f32[56,1152]{1,0:T(8,128)S(1)}, f32[56,1152]{1,0:T(8,128)S(1)}, f32[56,1152]{1,0:T(8,128)S(1)}, f32[4,8,512]{2,1,0:T(8,128)S(1)}, f32[8,8,512]{2,1,0:T(8,128)S(1)}) custom-call(f32[8,2,8,512]{3,2,1,0:T(8,128)S(1)} %all-to-all-done.refs_0_, bf16[544,288]{1,0:T(8,128)(2,1)S(1)} %copy-done, bf16[512,512]{1,0:T(8,128)(2,1)S(1)} %get-tuple-element.39.refs_2_, ...), custom_call_target="tpu_custom_call" | custom-call | tf_op jit(solution)/shard_map/middle/pallas_call | solution.py:442
  43.1 1.9 %collective-permute-start.1 = (f32[4,8,512]{2,1,0:T(8,128)S(1)}, f32[4,8,512]{2,1,0:T(8,128)S(1)}, u32[]{:S(2)}, u32[]{:S(2)}) collective-permute-start(f32[4,8,512]{2,1,0:T(8,128)S(1)} %get-tuple-element.44), channel_id=1, source_target_pairs={{4,8},{8,4},{5,9},{9,5},{6,10},{10,6},{7,11},{11,7},{12,16},{16,12... | collective-permute-start | bytes 196616 | tf_op jit(solution)/shard_map/ppermute | solution.py:486
  45.0 0.0 copy-done.4
  45.0 0.0 copy-done.8
  45.1 1.2 %own_b.1.refs_3_.refs_6_ = f32[56,1152]{1,0:T(8,128)S(1)} custom-call(f32[56,1152]{1,0:T(8,128)S(1)} %get-tuple-element.45.refs_0_, bf16[544,288]{1,0:T(8,128)(2,1)S(1)} %copy-done, f32[81,4,128]{2,1,0:T(4,128)S(1)} %bitcast.25, bf16[2,56,96]{2,1,0:T(8,128)(2,1)S(1)} %copy-done.8, f32[243,128]{1,0:T(8,128)S(1)} %copy-done.1, ...), custom_call_target="tpu_custom_call" | custom-call | tf_op jit(solution)/shard_map/own_b/pallas_call | solution.py:442
  46.2 2.5 %collective-permute-done.1 = f32[4,8,512]{2,1,0:T(8,128)S(1)} collective-permute-done((f32[4,8,512]{2,1,0:T(8,128)S(1)}, f32[4,8,512]{2,1,0:T(8,128)S(1)}, u32[]{:S(2)}, u32[]{:S(2)}) %collective-permute-start.1) | collective-permute-done | bytes 65568 | tf_op jit(solution)/shard_map/ppermute | solution.py:486
  48.7 0.0 copy-start.6
  48.7 0.7 %pad_maximum_fusion.1 = f32[8,2,8,512]{3,2,1,0:T(8,128)} fusion(f32[8,1,8,512]{3,2,1,0:T(8,128)S(1)} %maximum_bitcast_fusion.1, f32[8,1,8,512]{3,2,1,0:T(8,128)S(1)} %bitcast.26), kind=kLoop, calls=%fused_computation.1 | loop fusion | flops 65536 | bytes 524288 | tf_op jit(solution)/shard_map/stack | solution.py:491
  49.5 7.0 %all-to-all-start.1 = ((f32[8,2,8,512]{3,2,1,0:T(8,128)}), f32[8,2,8,512]{3,2,1,0:T(8,128)S(1)}, u32[]{:S(2)}, u32[]{:S(2)}) async-start(f32[8,2,8,512]{3,2,1,0:T(8,128)} %pad_maximum_fusion.1), calls=%async_computation.1 | async-start | bytes 524288 | tf_op jit(solution)/shard_map/all_to_all | solution.py:492
  56.4 0.0 copy-done.6
  56.4 0.6 pick_b.1.refs_3_
  57.0 6.0 %all-to-all-done.1.refs_0_ = f32[8,2,8,512]{3,2,1,0:T(8,128)S(1)} async-done(((f32[8,2,8,512]{3,2,1,0:T(8,128)}), f32[8,2,8,512]{3,2,1,0:T(8,128)S(1)}, u32[]{:S(2)}, u32[]{:S(2)}) %all-to-all-start.1) | async-done | bytes 262176 | tf_op jit(solution)/shard_map/all_to_all | solution.py:492
  63.0 2.2 %final.1 = f32[9,56,128]{2,1,0:T(8,128)} custom-call(f32[8,2,8,512]{3,2,1,0:T(8,128)S(1)} %all-to-all-done.1.refs_0_, bf16[544,288]{1,0:T(8,128)(2,1)S(1)} %copy-done, bf16[512,512]{1,0:T(8,128)(2,1)S(1)} %get-tuple-element.39.refs_2_, f32[224,512]{1,0:T(8,128)S(1)} %pick_b.1.refs_3_, f32[81,4,128]{2,1,0:T(4,128)S(1)} %bitcast.23, ...), custom_call_target="tpu_custom_call" | custom-call | tf_op jit(solution)/shard_map/final/pallas_call | solution.py:442
  (2 shorter events, 0.0 us)
Async XLA Ops:
  6.8 8.7 %collective-permute-start = (f32[4,8,512]{2,1,0:T(8,128)}, f32[4,8,512]{2,1,0:T(8,128)S(1)}, u32[]{:S(2)}, u32[]{:S(2)}) collective-permute-start(f32[4,8,512]{2,1,0:T(8,128)} %get-tuple-element.30), channel_id=1, source_target_pairs={{4,8},{8,4},{5,9},{9,5},{6,10},{10,6},{7,11},{11,7},{12,16},{16,12... | collective-permute-start | bytes 196616 | tf_op jit(solution)/shard_map/ppermute | solution.py:486
  11.4 4.2 %copy-start.14 = (f32[8,8,512]{2,1,0:T(8,128)S(1)}, f32[8,8,512]{2,1,0:T(8,128)}, u32[]{:S(2)}) copy-start(f32[8,8,512]{2,1,0:T(8,128)} %get-tuple-element.29) | copy-start | bytes 393220
  11.4 19.4 %copy-start.9 = (s32[4,128]{1,0:T(4,128)S(1)}, s32[4,128]{1,0:T(4,128)}, u32[]{:S(2)}) copy-start(s32[4,128]{1,0:T(4,128)} %refs_0_.3) | copy-start | bytes 6148
  11.4 19.4 %copy-start.10 = (s32[4,128]{1,0:T(4,128)S(1)}, s32[4,128]{1,0:T(4,128)}, u32[]{:S(2)}) copy-start(s32[4,128]{1,0:T(4,128)} %refs_1_.1) | copy-start | bytes 6148
  11.4 19.3 %copy-start.11 = (s32[4,128]{1,0:T(4,128)S(1)}, s32[4,128]{1,0:T(4,128)}, u32[]{:S(2)}) copy-start(s32[4,128]{1,0:T(4,128)} %refs_3_.5) | copy-start | bytes 6148
  11.5 19.3 %copy-start.12 = (s32[96]{0:T(128)S(1)}, s32[96]{0:T(128)}, u32[]{:S(2)}) copy-start(s32[96]{0:T(128)} %param.29) | copy-start | bytes 1156
  11.5 19.3 %copy-start.13 = (s32[128]{0:T(128)S(1)}, s32[128]{0:T(128)}, u32[]{:S(2)}) copy-start(s32[128]{0:T(128)} %param.25) | copy-start | bytes 1540
  11.5 25.8 %copy-start.3 = (f32[4,9,9,128]{3,0,2,1:T(4,128)S(1)}, f32[4,9,9,128]{3,0,2,1:T(4,128)}, u32[]{:S(2)}) copy-start(f32[4,9,9,128]{3,0,2,1:T(4,128)} %param.24) | copy-start | bytes 497668
  15.6 21.8 %copy-start.2 = (f32[224,1152]{1,0:T(8,128)S(1)}, f32[224,1152]{1,0:T(8,128)}, u32[]{:S(2)}) copy-start(f32[224,1152]{1,0:T(8,128)} %get-tuple-element.42.refs_6_) | copy-start | bytes 3096580
  16.3 21.0 %copy-start = (bf16[544,288]{1,0:T(8,128)(2,1)S(1)}, bf16[544,288]{1,0:T(8,128)(2,1)}, u32[]{:S(2)}) copy-start(bf16[544,288]{1,0:T(8,128)(2,1)} %get-tuple-element.37.refs_1_) | copy-start | bytes 940036
  16.3 21.0 %all-to-all-start = ((f32[8,2,8,512]{3,2,1,0:T(8,128)}), f32[8,2,8,512]{3,2,1,0:T(8,128)S(1)}, u32[]{:S(2)}, u32[]{:S(2)}) async-start(f32[8,2,8,512]{3,2,1,0:T(8,128)} %pad_maximum_fusion), calls=%async_computation | async-start | bytes 524288 | tf_op jit(solution)/shard_map/all_to_all | solution.py:492
  30.8 1.0 %copy-start.7 = (f32[96,1152]{1,0:T(8,128)S(1)}, f32[96,1152]{1,0:T(8,128)}, u32[]{:S(2)}) copy-start(f32[96,1152]{1,0:T(8,128)} %get-tuple-element.38.refs_2_) | copy-start | bytes 1327108
  31.8 5.5 %copy-start.1 = (f32[243,128]{1,0:T(8,128)S(1)}, f32[243,128]{1,0:T(8,128)}, u32[]{:S(2)}) copy-start(f32[243,128]{1,0:T(8,128)} %get-tuple-element.32.refs_6_.refs_7_.refs_4_) | copy-start | bytes 373252
  32.4 0.8 %copy-start.5 = (bf16[512,512]{1,0:T(8,128)(2,1)}, bf16[512,512]{1,0:T(8,128)(2,1)S(1)}, u32[]{:S(2)}) copy-start(bf16[512,512]{1,0:T(8,128)(2,1)S(1)} %get-tuple-element.51.refs_2_) | copy-start | bytes 1572868
  37.3 7.7 %copy-start.4 = (f32[4,9,9,128]{3,0,2,1:T(4,128)S(1)}, f32[4,9,9,128]{3,0,2,1:T(4,128)}, u32[]{:S(2)}) copy-start(f32[4,9,9,128]{3,0,2,1:T(4,128)} %param.23) | copy-start | bytes 497668
  37.3 7.7 %copy-start.8 = (bf16[2,56,96]{2,1,0:T(8,128)(2,1)S(1)}, bf16[2,56,96]{2,1,0:T(8,128)(2,1)}, u32[]{:S(2)}) copy-start(bf16[2,56,96]{2,1,0:T(8,128)(2,1)} %get-tuple-element.46.refs_3_) | copy-start | bytes 64516
  43.1 5.6 %collective-permute-start.1 = (f32[4,8,512]{2,1,0:T(8,128)S(1)}, f32[4,8,512]{2,1,0:T(8,128)S(1)}, u32[]{:S(2)}, u32[]{:S(2)}) collective-permute-start(f32[4,8,512]{2,1,0:T(8,128)S(1)} %get-tuple-element.44), channel_id=1, source_target_pairs={{4,8},{8,4},{5,9},{9,5},{6,10},{10,6},{7,11},{11,7},{12,16},{16,12... | collective-permute-start | bytes 196616 | tf_op jit(solution)/shard_map/ppermute | solution.py:486
  48.7 7.7 %copy-start.6 = (bf16[512,512]{1,0:T(8,128)(2,1)S(1)}, bf16[512,512]{1,0:T(8,128)(2,1)}, u32[]{:S(2)}) copy-start(bf16[512,512]{1,0:T(8,128)(2,1)} %copy-done.5) | copy-start | bytes 1572868
  49.5 13.5 %all-to-all-start.1 = ((f32[8,2,8,512]{3,2,1,0:T(8,128)}), f32[8,2,8,512]{3,2,1,0:T(8,128)S(1)}, u32[]{:S(2)}, u32[]{:S(2)}) async-start(f32[8,2,8,512]{3,2,1,0:T(8,128)} %pad_maximum_fusion.1), calls=%async_computation.1 | async-start | bytes 524288 | tf_op jit(solution)/shard_map/all_to_all | solution.py:492
